TPU v7x, 32 devices: a whole 2x2x4 slice. The times are simulated.
32 devices in a mesh: group: 2 (over x), frame: 4 (over y, core), row: 4 (over z).
Axes of the slice: x: 2, y: 2, z: 4, core: 2. Of those that a mesh axis runs over, the one named last changes fastest.
Arguments:
- latents: bfloat16 [48, 8, 64, 320], P(('group', 'frame'), 'row'), parts along dimension 0, may hold values from -8 to 8
- condition: bfloat16 [24, 8, 64, 320], P(('group', 'frame'), 'row'), parts along dimension 0, may hold values from -6 to 6
- key_frames: int32 [24], P('group'), parts along dimension 0, may hold values from -1 to 23, as said below
- propagate: int32 [48], P('group'), parts along dimension 0, may hold values from 0 to 11, as said below
- encoder_conv: bfloat16 [9, 320, 320], replicated, may hold values from -0.109375 to 0.109375
- zero_conv: bfloat16 [320, 320], replicated, may hold values from -0.3125 to 0.3125
- attention_gain: float32 [320], replicated, may hold values from 0.25 to 1.75
- query_weight: bfloat16 [320, 320], replicated, may hold values from -3 to 3
- key_weight: bfloat16 [320, 320], replicated, may hold values from -3 to 3
- value_weight: bfloat16 [320, 320], replicated, may hold values from -0.3125 to 0.3125
- output_weight: bfloat16 [320, 320], replicated, may hold values from -0.3125 to 0.3125
- conv_gain: float32 [320], replicated, may hold values from 0.25 to 1.75
- block_conv: bfloat16 [9, 320, 320], replicated, may hold values from -0.109375 to 0.109375
Outputs:
- updated: bfloat16 [48, 8, 64, 320], P(('group', 'frame'), 'row'), parts along dimension 0
There are 2 independent parts, one for each index of `group`. A program takes and returns all parts, laid end to end along the dimension named above; an argument that names none is the same for every part. Nothing has to cross between parts.
Inputs may be any that keep to these rules, and one draw needn't show every extreme that they name: `key_frames`: the 3 slots of index d of frame hold keyframes of frames d * 6 to (d + 1) * 6 - 1, all different, live slots first; of index d and the index half the frame axis away, one holds 3 live keyframes and the other 1. `propagate`: each frame names a live slot of its own index of frame or of an adjacent one (no wrap); a keyframe's own frame names its own slot.
All inputs are finite; a program needn't handle non-finite values.
Results may differ from a plain program's by a relative error of at most 0.014.
Values may be sent and summed in bfloat16 or wider, within the bound.
No kernel may reach another device: no remote copies, remote signals or barrier semaphores. Data moves between devices by JAX's collectives and lax.ppermute only.
A program may use at most 64 MiB of HBM per device.

v0:
```python
import math

import jax
import jax.numpy as jnp
from jax import lax
from jax.sharding import PartitionSpec as P

HEADS = 8


def extended(shard, sides, width):
    for axis, dim in sides:
        size, length = (lax.axis_size(axis), shard.shape[dim])
        up = [(i, (i + 1) % size) for i in range(size - 1)]
        down = [(j, i) for i, j in up]
        last = lax.slice_in_dim(shard, length - width, length, axis=dim)
        initial = lax.slice_in_dim(shard, 0, width, axis=dim)
        before = lax.ppermute(last, axis, up)
        after = lax.ppermute(initial, axis, down)
        shard = jnp.concatenate([before, shard, after], axis=dim)
    return shard


def layer_norm(values_in, scale_gain):
    average = jnp.mean(values_in, axis=-1, keepdims=True)
    centered = values_in - average
    variance = jnp.mean(centered * centered, axis=-1, keepdims=True)
    return centered * lax.rsqrt(variance + 1e-05) * scale_gain


def positions(frame_total, channels):
    frame_pos = jnp.arange(frame_total, dtype=jnp.float32)[:, None]
    half_index = jnp.arange(channels // 2, dtype=jnp.float32)
    frequency = jnp.exp(half_index * (-2.0 * math.log(10000.0) / channels))
    angles = frame_pos * frequency
    return jnp.stack([jnp.sin(angles), jnp.cos(angles)], axis=-1).reshape(frame_total, channels)


def conv_taps(padded, weights):
    slab_count, padded_rows, col_count, channels = padded.shape
    row_count = padded_rows - 2
    widened = jnp.pad(padded, ((0, 0), (0, 0), (1, 1), (0, 0)))
    running = jnp.zeros((slab_count * row_count * col_count, weights.shape[2]), jnp.float32)
    for row_off in range(3):
        for col_off in range(3):
            window = widened[
                :, row_off : row_off + row_count, col_off : col_off + col_count, :
            ].reshape(-1, channels)
            running = running + jnp.dot(
                window, weights[3 * row_off + col_off], preferred_element_type=jnp.float32
            )
    return running.reshape(slab_count, row_count, col_count, -1)


def shards(
    latents,
    condition,
    key_frames,
    propagate,
    encoder_conv,
    zero_conv,
    attention_gain,
    query_weight,
    key_weight,
    value_weight,
    output_weight,
    conv_gain,
    block_conv,
):
    frames_dev = latents.shape[0]
    channels = latents.shape[3]
    slot_count = condition.shape[0]
    head_dim = channels // HEADS
    axis_len = lax.axis_size("frame")
    total_frames = frames_dev * axis_len
    total_slots = slot_count * axis_len
    padded = extended(condition, (("row", 1),), 1)
    features = jax.nn.silu(conv_taps(padded, encoder_conv)).astype(jnp.bfloat16)
    projected = jnp.dot(
        features.reshape(-1, channels), zero_conv, preferred_element_type=jnp.float32
    )
    keyres = projected.astype(jnp.bfloat16).reshape(condition.shape)
    encoding = positions(total_frames, channels)
    latents_pix = lax.all_to_all(latents, "frame", split_axis=2, concat_axis=0, tiled=True)
    residual_pix = lax.all_to_all(keyres, "frame", split_axis=2, concat_axis=0, tiled=True)
    all_frames = jnp.arange(total_frames, dtype=jnp.int32)
    onehot = (
        propagate[:, None] - 0 == jnp.arange(residual_pix.shape[0], dtype=jnp.int32)[None, :]
    ).astype(jnp.bfloat16)
    picked = jnp.dot(
        onehot, residual_pix.reshape(residual_pix.shape[0], -1), preferred_element_type=jnp.float32
    ).reshape(latents_pix.shape)
    source_frame = jnp.sum(
        jnp.where(
            propagate[:, None] == jnp.arange(total_slots, dtype=jnp.int32)[None, :],
            key_frames[None, :],
            0,
        ),
        axis=1,
    )
    reach = jnp.exp(-jnp.abs(all_frames - source_frame).astype(jnp.float32) / (2 * frames_dev))
    hidden_pix = (latents_pix.astype(jnp.float32) + reach[:, None, None, None] * picked).astype(
        jnp.bfloat16
    )
    frame_count, row_count, col_count, _ = hidden_pix.shape
    normed = (
        layer_norm(hidden_pix.astype(jnp.float32), attention_gain) + encoding[:, None, None, :]
    ).astype(jnp.bfloat16)
    flattened = normed.reshape(-1, channels)
    head_shape = (frame_count, row_count * col_count, HEADS, head_dim)
    query = (
        jnp.dot(flattened, query_weight, preferred_element_type=jnp.float32)
        .astype(jnp.bfloat16)
        .reshape(head_shape)
    )
    key_proj = (
        jnp.dot(flattened, key_weight, preferred_element_type=jnp.float32)
        .astype(jnp.bfloat16)
        .reshape(head_shape)
    )
    value_proj = (
        jnp.dot(flattened, value_weight, preferred_element_type=jnp.float32)
        .astype(jnp.bfloat16)
        .reshape(head_shape)
    )
    scores = jnp.einsum(
        "fphd,gphd->phfg", query, key_proj, preferred_element_type=jnp.float32
    ) / math.sqrt(head_dim)
    weights_soft = jax.nn.softmax(scores, axis=-1).astype(jnp.bfloat16)
    mixed_heads = (
        jnp.einsum("phfg,gphd->fphd", weights_soft, value_proj, preferred_element_type=jnp.float32)
        .astype(jnp.bfloat16)
        .reshape(-1, channels)
    )
    projected = jnp.dot(mixed_heads, output_weight, preferred_element_type=jnp.float32)
    attended_pix = (
        (hidden_pix.astype(jnp.float32).reshape(-1, channels) + projected)
        .astype(jnp.bfloat16)
        .reshape(hidden_pix.shape)
    )
    attended = lax.all_to_all(attended_pix, "frame", split_axis=0, concat_axis=2, tiled=True)
    activated = jax.nn.silu(layer_norm(attended.astype(jnp.float32), conv_gain)).astype(
        jnp.bfloat16
    )
    padded_rows = extended(activated, (("row", 1),), 1)
    convolved = conv_taps(padded_rows, block_conv)
    return (attended.astype(jnp.float32) + convolved).astype(jnp.bfloat16)


def solution(mesh):
    placed = (
        P(("group", "frame"), "row", None, None),
        P(("group", "frame"), "row", None, None),
        P("group"),
        P("group"),
        P(),
        P(),
        P(),
        P(),
        P(),
        P(),
        P(),
        P(),
        P(),
    )
    return jax.shard_map(
        shards,
        mesh=mesh,
        in_specs=placed,
        out_specs=P(("group", "frame"), "row", None, None),
        check_vma=False,
    )
```

profile of v0, /device:TPU:8, one launch (start us, length us, event | category | flops | bytes accessed | tf_op | source)
XLA Modules:
  0.0 117.6 jit_solution(18311225892279663839)
XLA Ops:
  0.0 1.1 fusion.84
  1.1 3.5 %collective-permute-start = (bf16[3,1,64,320]{3,2,1,0:T(8,128)(2,1)S(1)}, bf16[3,1,64,320]{3,2,1,0:T(8,128)(2,1)S(1)}, u32[]{:S(2)}, u32[]{:S(2)}) collective-permute-start(bf16[3,1,64,320]{3,2,1,0:T(8,128)(2,1)S(1)} %get-tuple-element.23), channel_id=1, source_target_pairs={{0,1},{1,2},{2,3},{4,5},{5,6},{6,7},{8,9},{9,10},{10,11},{12,13},{... | collective-permute-start | bytes 368648 | tf_op jit(solution)/shard_map/ppermute | solution.py:18
  4.6 2.4 %collective-permute-start.1 = (bf16[3,1,64,320]{3,2,1,0:T(8,128)(2,1)S(1)}, bf16[3,1,64,320]{3,2,1,0:T(8,128)(2,1)S(1)}, u32[]{:S(2)}, u32[]{:S(2)}) collective-permute-start(bf16[3,1,64,320]{3,2,1,0:T(8,128)(2,1)S(1)} %get-tuple-element.24), channel_id=1, source_target_pairs={{1,0},{2,1},{3,2},{5,4},{6,5},{7,6},{9,8},{10,9},{11,10},{13,12},{... | collective-permute-start | bytes 368648 | tf_op jit(solution)/shard_map/ppermute | solution.py:19
  6.9 2.3 %copy.87 = bf16[6,2,64,320]{3,0,1,2:T(8,128)(2,1)} copy(bf16[6,2,64,320]{3,2,1,0:T(8,128)(2,1)} %param.13) | data formatting | bytes 983040 | tf_op args[0]
  9.3 2.5 %collective-permute-done.1 = bf16[3,1,64,320]{3,2,1,0:T(8,128)(2,1)S(1)} collective-permute-done((bf16[3,1,64,320]{3,2,1,0:T(8,128)(2,1)S(1)}, bf16[3,1,64,320]{3,2,1,0:T(8,128)(2,1)S(1)}, u32[]{:S(2)}, u32[]{:S(2)}) %collective-permute-start.1) | collective-permute-done | bytes 122912 | tf_op jit(solution)/shard_map/ppermute | solution.py:19
  12.3 1.3 %copy-done.5 = bf16[9,320,320]{2,1,0:T(8,128)(2,1)S(1)} copy-done((bf16[9,320,320]{2,1,0:T(8,128)(2,1)S(1)}, bf16[9,320,320]{2,1,0:T(8,128)(2,1)}, u32[]{:S(2)}) %copy-start.5) | copy-done | bytes 1843224
  17.0 1.7 %convolution_convert_fusion.4 = bf16[384,320]{0,1:T(8,128)(2,1)S(1)} fusion(bf16[320,320]{1,0:T(8,128)(2,1)S(1)} %copy-done.11, f32[384,320]{0,1:T(8,128)S(1)} %fusion.40, f32[384,320]{0,1:T(8,128)S(1)} %convolution_add_fusion.9, bf16[384,320]{1,0:T(8,128)(2,1)S(1)} %bitcast.195, bf16[9,320,320]{2,1,0:T(8,128)(2,1)} %param.17), kind=kOutput, calls=%fused_computation.45 | convolution fusion | flops 158269440 | bytes 1925120 | tf_op jit(solution)/shard_map/dot_general | solution.py:79
  18.9 1.0 copy.91
  19.9 3.6 %all-to-all-start.1 = ((bf16[3,2,64,320]{3,1,0,2:T(2,128)(2,1)}), bf16[3,2,64,320]{3,1,0,2:T(2,128)(2,1)S(1)}, u32[]{:S(2)}, u32[]{:S(2)}) async-start(bf16[3,2,64,320]{3,1,0,2:T(2,128)(2,1)} %copy.91), calls=%async_computation.1 | async-start | bytes 589824 | tf_op jit(solution)/shard_map/all_to_all | solution.py:85
  23.6 6.2 %all-to-all-done.1 = bf16[3,2,64,320]{3,1,0,2:T(2,128)(2,1)S(1)} async-done(((bf16[3,2,64,320]{3,1,0,2:T(2,128)(2,1)}), bf16[3,2,64,320]{3,1,0,2:T(2,128)(2,1)S(1)}, u32[]{:S(2)}, u32[]{:S(2)}) %all-to-all-start.1) | async-done | bytes 245792 | tf_op jit(solution)/shard_map/all_to_all | solution.py:85
  29.8 3.7 %all-to-all-start = ((bf16[6,2,64,320]{3,0,1,2:T(8,128)(2,1)}), bf16[6,2,64,320]{3,0,1,2:T(8,128)(2,1)S(1)}, u32[]{:S(2)}, u32[]{:S(2)}) async-start(bf16[6,2,64,320]{3,0,1,2:T(8,128)(2,1)} %copy.87), calls=%async_computation | async-start | bytes 1572864 | tf_op jit(solution)/shard_map/all_to_all | solution.py:84
  34.7 10.3 %all-to-all-done = bf16[6,2,64,320]{3,0,1,2:T(8,128)(2,1)S(1)} async-done(((bf16[6,2,64,320]{3,0,1,2:T(8,128)(2,1)}), bf16[6,2,64,320]{3,0,1,2:T(8,128)(2,1)S(1)}, u32[]{:S(2)}, u32[]{:S(2)}) %all-to-all-start) | async-done | bytes 491552 | tf_op jit(solution)/shard_map/all_to_all | solution.py:84
  46.3 1.3 %copy.96 = f32[24,2,16,320]{3,2,1,0:T(8,128)} copy(f32[24,2,16,320]{3,0,2,1:T(8,128)S(1)} %get-tuple-element.28) | data formatting | bytes 1966080 | tf_op jit(solution)/shard_map/convert_element_type | solution.py:137
  48.8 1.4 %reshape.271 = bf16[24,32,8,40]{1,0,3,2:T(8,128)(2,1)S(1)} reshape(bf16[768,320]{0,1:T(8,128)(2,1)S(1)} %convolution_convert_fusion.2) | data formatting | bytes 983040 | tf_op jit(solution)/shard_map/reshape | solution.py:114
  50.2 3.9 %copy.103 = bf16[24,32,8,40]{3,0,2,1:T(8,128)(2,1)} copy(bf16[24,32,8,40]{1,0,3,2:T(8,128)(2,1)S(1)} %reshape.271) | data formatting | bytes 983040 | tf_op jit(solution)/shard_map/reshape | solution.py:114
  54.1 1.4 %convolution_convert_fusion.1 = bf16[768,320]{0,1:T(8,128)(2,1)S(1)} fusion(bf16[768,320]{1,0:T(8,128)(2,1)S(1)} %bitcast.167, bf16[320,320]{1,0:T(8,128)(2,1)} %param.21), kind=kOutput, calls=%fused_computation.33 | convolution fusion | flops 157532160 | bytes 1187840 | tf_op jit(solution)/shard_map/dot_general | solution.py:117
  55.5 1.4 %reshape.272 = bf16[24,32,8,40]{1,0,3,2:T(8,128)(2,1)S(1)} reshape(bf16[768,320]{0,1:T(8,128)(2,1)S(1)} %convolution_convert_fusion.1) | data formatting | bytes 983040 | tf_op jit(solution)/shard_map/reshape | solution.py:119
  56.9 3.9 %copy.104 = bf16[24,32,8,40]{3,0,2,1:T(8,128)(2,1)} copy(bf16[24,32,8,40]{1,0,3,2:T(8,128)(2,1)S(1)} %reshape.272) | data formatting | bytes 983040 | tf_op jit(solution)/shard_map/reshape | solution.py:119
  60.9 1.4 %convolution_convert_fusion.3 = bf16[768,320]{0,1:T(8,128)(2,1)S(1)} fusion(bf16[768,320]{1,0:T(8,128)(2,1)S(1)} %bitcast.168, bf16[320,320]{1,0:T(8,128)(2,1)} %param.22), kind=kOutput, calls=%fused_computation.35 | convolution fusion | flops 157532160 | bytes 1187840 | tf_op jit(solution)/shard_map/dot_general | solution.py:122
  62.3 1.4 %reshape.270 = bf16[24,32,8,40]{1,0,3,2:T(8,128)(2,1)S(1)} reshape(bf16[768,320]{0,1:T(8,128)(2,1)S(1)} %convolution_convert_fusion.3) | data formatting | bytes 983040 | tf_op jit(solution)/shard_map/reshape | solution.py:124
  63.7 3.9 %copy.105 = bf16[24,32,8,40]{3,0,2,1:T(8,128)(2,1)} copy(bf16[24,32,8,40]{1,0,3,2:T(8,128)(2,1)S(1)} %reshape.270) | data formatting | bytes 983040 | tf_op jit(solution)/shard_map/reshape | solution.py:124
  67.6 5.4 %fusion.86 = (f32[32,8,24]{2,1,0:T(8,128)S(1)}, f32[32,8,24,24]{2,3,1,0:T(8,128)}) fusion(bf16[24,32,8,40]{3,0,2,1:T(8,128)(2,1)} %copy.103, bf16[24,32,8,40]{3,0,2,1:T(8,128)(2,1)} %copy.104), kind=kOutput, calls=%fused_computation.133 | convolution fusion | flops 12238871 | bytes 1597440 | tf_op jit(solution)/shard_map/sub | solution.py:129
  73.0 2.9 %fusion.10 = bf16[24,32,8,40]{3,0,2,1:T(8,128)(2,1)S(1)} fusion(bf16[24,32,8,40]{3,0,2,1:T(8,128)(2,1)S(1)} %copy-done.6, f32[32,8,24,24]{2,3,1,0:T(8,128)} %get-tuple-element.30, f32[32,8,24]{2,1,0:T(8,128)S(1)} %get-tuple-element.29), kind=kOutput, calls=%fused_computation.16 | convolution fusion | flops 12337152 | bytes 1597440 | tf_op jit(solution)/shard_map/phfg,gphd->fphd/dot_general | solution.py:131
  76.3 2.0 %reshape.253 = bf16[768,320]{1,0:T(8,128)(2,1)} reshape(bf16[24,32,8,40]{3,2,1,0:T(8,128)(2,1)S(1)} %copy.107) | data formatting | bytes 983040 | tf_op jit(solution)/shard_map/reshape | solution.py:133
  80.2 11.9 %all_to_all.33 = bf16[24,2,16,320]{3,2,1,0:T(8,128)(2,1)S(1)} all-to-all(bf16[24,2,16,320]{3,2,1,0:T(8,128)(2,1)S(1)} %bitcast.180), channel_id=1, replica_groups=mesh['group'=2,'frame'=4,'row'=4] {'frame'}, dimensions={0} | all-to-all | bytes 983040 | tf_op jit(solution)/shard_map/all_to_all | solution.py:141
  93.6 3.5 %collective-permute-start.2 = (bf16[6,1,64,320]{3,2,1,0:T(8,128)(2,1)S(1)}, bf16[6,1,64,320]{3,2,1,0:T(8,128)(2,1)S(1)}, u32[]{:S(2)}, u32[]{:S(2)}) collective-permute-start(bf16[6,1,64,320]{3,2,1,0:T(8,128)(2,1)S(1)} %get-tuple-element.19), channel_id=1, source_target_pairs={{0,1},{1,2},{2,3},{4,5},{5,6},{6,7},{8,9},{9,10},{10,11},{12,13},{... | collective-permute-start | bytes 737288 | tf_op jit(solution)/shard_map/ppermute | solution.py:18
  97.1 2.4 %collective-permute-start.3 = (bf16[6,1,64,320]{3,2,1,0:T(8,128)(2,1)S(1)}, bf16[6,1,64,320]{3,2,1,0:T(8,128)(2,1)S(1)}, u32[]{:S(2)}, u32[]{:S(2)}) collective-permute-start(bf16[6,1,64,320]{3,2,1,0:T(8,128)(2,1)S(1)} %get-tuple-element.20), channel_id=1, source_target_pairs={{1,0},{2,1},{3,2},{5,4},{6,5},{7,6},{9,8},{10,9},{11,10},{13,12},{... | collective-permute-start | bytes 737288 | tf_op jit(solution)/shard_map/ppermute | solution.py:19
  99.9 4.2 %collective-permute-done.2 = bf16[6,1,64,320]{3,2,1,0:T(8,128)(2,1)S(1)} collective-permute-done((bf16[6,1,64,320]{3,2,1,0:T(8,128)(2,1)S(1)}, bf16[6,1,64,320]{3,2,1,0:T(8,128)(2,1)S(1)}, u32[]{:S(2)}, u32[]{:S(2)}) %collective-permute-start.2) | collective-permute-done | bytes 245792 | tf_op jit(solution)/shard_map/ppermute | solution.py:18
  104.2 3.2 %collective-permute-done.3 = bf16[6,1,64,320]{3,2,1,0:T(8,128)(2,1)S(1)} collective-permute-done((bf16[6,1,64,320]{3,2,1,0:T(8,128)(2,1)S(1)}, bf16[6,1,64,320]{3,2,1,0:T(8,128)(2,1)S(1)}, u32[]{:S(2)}, u32[]{:S(2)}) %collective-permute-start.3) | collective-permute-done | bytes 245792 | tf_op jit(solution)/shard_map/ppermute | solution.py:19
  113.6 1.4 %fusion.12 = f32[768,320]{0,1:T(8,128)} fusion(f32[768,320]{0,1:T(8,128)S(1)} %fusion.29, f32[768,320]{0,1:T(8,128)S(1)} %convolution_add_fusion.1, bf16[768,320]{1,0:T(8,128)(2,1)S(1)} %bitcast.183, bf16[9,320,320]{2,1,0:T(8,128)(2,1)S(1)} %copy-done.4), kind=kOutput, calls=%fused_computation.20 | convolution fusion | flops 157777920 | bytes 3784704 | tf_op jit(solution)/shard_map/dot_general | solution.py:49
  115.1 1.6 %copy.111 = f32[768,320]{1,0:T(8,128)S(1)} copy(f32[768,320]{0,1:T(8,128)} %fusion.12) | data formatting | bytes 1966080 | tf_op jit(solution)/shard_map/add | solution.py:49
  116.6 1.0 fusion.22
  (84 shorter events, 18.0 us)
Async XLA Ops:
  0.0 48.4 %copy-start = (bf16[320,320]{1,0:T(8,128)(2,1)S(1)}, bf16[320,320]{1,0:T(8,128)(2,1)}, u32[]{:S(2)}) copy-start(bf16[320,320]{1,0:T(8,128)(2,1)} %param.20) | copy-start | bytes 614404
  0.0 11.8 %copy-start.2 = (bf16[3,2,64,320]{3,2,1,0:T(8,128)(2,1)S(1)}, bf16[3,2,64,320]{3,2,1,0:T(8,128)(2,1)}, u32[]{:S(2)}) copy-start(bf16[3,2,64,320]{3,2,1,0:T(8,128)(2,1)} %param.14) | copy-start | bytes 737284
  1.1 8.2 %collective-permute-start = (bf16[3,1,64,320]{3,2,1,0:T(8,128)(2,1)S(1)}, bf16[3,1,64,320]{3,2,1,0:T(8,128)(2,1)S(1)}, u32[]{:S(2)}, u32[]{:S(2)}) collective-permute-start(bf16[3,1,64,320]{3,2,1,0:T(8,128)(2,1)S(1)} %get-tuple-element.23), channel_id=1, source_target_pairs={{0,1},{1,2},{2,3},{4,5},{5,6},{6,7},{8,9},{9,10},{10,11},{12,13},{... | collective-permute-start | bytes 368648 | tf_op jit(solution)/shard_map/ppermute | solution.py:18
  4.6 7.2 %collective-permute-start.1 = (bf16[3,1,64,320]{3,2,1,0:T(8,128)(2,1)S(1)}, bf16[3,1,64,320]{3,2,1,0:T(8,128)(2,1)S(1)}, u32[]{:S(2)}, u32[]{:S(2)}) collective-permute-start(bf16[3,1,64,320]{3,2,1,0:T(8,128)(2,1)S(1)} %get-tuple-element.24), channel_id=1, source_target_pairs={{1,0},{2,1},{3,2},{5,4},{6,5},{7,6},{9,8},{10,9},{11,10},{13,12},{... | collective-permute-start | bytes 368648 | tf_op jit(solution)/shard_map/ppermute | solution.py:19
  12.0 1.6 %copy-start.5 = (bf16[9,320,320]{2,1,0:T(8,128)(2,1)S(1)}, bf16[9,320,320]{2,1,0:T(8,128)(2,1)}, u32[]{:S(2)}) copy-start(bf16[9,320,320]{2,1,0:T(8,128)(2,1)} %param.17) | copy-start | bytes 5529604
  16.1 0.9 copy-start.11
  19.9 13.8 %copy-start.10 = (s32[24]{0:T(128)S(1)}, s32[24]{0:T(128)}, u32[]{:S(2)}) copy-start(s32[24]{0:T(128)} %param.16) | copy-start | bytes 292
  19.9 13.8 %copy-start.12 = (s32[12]{0:T(128)S(1)}, s32[12]{0:T(128)}, u32[]{:S(2)}) copy-start(s32[12]{0:T(128)} %param.15) | copy-start | bytes 148
  19.9 9.9 %all-to-all-start.1 = ((bf16[3,2,64,320]{3,1,0,2:T(2,128)(2,1)}), bf16[3,2,64,320]{3,1,0,2:T(2,128)(2,1)S(1)}, u32[]{:S(2)}, u32[]{:S(2)}) async-start(bf16[3,2,64,320]{3,1,0,2:T(2,128)(2,1)} %copy.91), calls=%async_computation.1 | async-start | bytes 589824 | tf_op jit(solution)/shard_map/all_to_all | solution.py:85
  29.8 15.1 %all-to-all-start = ((bf16[6,2,64,320]{3,0,1,2:T(8,128)(2,1)}), bf16[6,2,64,320]{3,0,1,2:T(8,128)(2,1)S(1)}, u32[]{:S(2)}, u32[]{:S(2)}) async-start(bf16[6,2,64,320]{3,0,1,2:T(8,128)(2,1)} %copy.87), calls=%async_computation | async-start | bytes 1572864 | tf_op jit(solution)/shard_map/all_to_all | solution.py:84
  46.3 1.7 %copy-start.9 = (f32[320]{0:T(512)S(1)}, f32[320]{0:T(512)}, u32[]{:S(2)}) copy-start(f32[320]{0:T(512)} %param.19) | copy-start | bytes 3844
  67.6 5.4 %copy-start.6 = (bf16[24,32,8,40]{3,0,2,1:T(8,128)(2,1)S(1)}, bf16[24,32,8,40]{3,0,2,1:T(8,128)(2,1)}, u32[]{:S(2)}) copy-start(bf16[24,32,8,40]{3,0,2,1:T(8,128)(2,1)} %copy.105) | copy-start | bytes 1474564
  76.3 2.0 %copy-start.1 = (f32[24,2,16,320]{3,2,1,0:T(8,128)S(1)}, f32[24,2,16,320]{3,2,1,0:T(8,128)}, u32[]{:S(2)}) copy-start(f32[24,2,16,320]{3,2,1,0:T(8,128)} %copy.96) | copy-start | bytes 2949124
  78.3 1.1 copy-start.3
  78.3 1.1 copy-start.7
  92.3 0.8 copy-start.8
  93.6 10.6 %collective-permute-start.2 = (bf16[6,1,64,320]{3,2,1,0:T(8,128)(2,1)S(1)}, bf16[6,1,64,320]{3,2,1,0:T(8,128)(2,1)S(1)}, u32[]{:S(2)}, u32[]{:S(2)}) collective-permute-start(bf16[6,1,64,320]{3,2,1,0:T(8,128)(2,1)S(1)} %get-tuple-element.19), channel_id=1, source_target_pairs={{0,1},{1,2},{2,3},{4,5},{5,6},{6,7},{8,9},{9,10},{10,11},{12,13},{... | collective-permute-start | bytes 737288 | tf_op jit(solution)/shard_map/ppermute | solution.py:18
  97.1 10.3 %collective-permute-start.3 = (bf16[6,1,64,320]{3,2,1,0:T(8,128)(2,1)S(1)}, bf16[6,1,64,320]{3,2,1,0:T(8,128)(2,1)S(1)}, u32[]{:S(2)}, u32[]{:S(2)}) collective-permute-start(bf16[6,1,64,320]{3,2,1,0:T(8,128)(2,1)S(1)} %get-tuple-element.20), channel_id=1, source_target_pairs={{1,0},{2,1},{3,2},{5,4},{6,5},{7,6},{9,8},{10,9},{11,10},{13,12},{... | collective-permute-start | bytes 737288 | tf_op jit(solution)/shard_map/ppermute | solution.py:19
  108.0 1.6 %copy-start.4 = (bf16[9,320,320]{2,1,0:T(8,128)(2,1)S(1)}, bf16[9,320,320]{2,1,0:T(8,128)(2,1)}, u32[]{:S(2)}) copy-start(bf16[9,320,320]{2,1,0:T(8,128)(2,1)} %param.25) | copy-start | bytes 5529604
where the time goes:
time: 120 us; the launch traced here: 118 us
  local copies, waits for them, and re-layouts  32.3 us (27%)
  waiting for transfers between devices  26.4 us (22%)
  matrix products  22.9 us (19%)
  starting transfers between devices  19 us (16%)
  blocking collectives  11.9 us (10%)
  other arithmetic  4.6 us (4%)
    all_to_all x1, blocking collectives, shards(): lax.all_to_all(attended_pix, 'frame', split_axis=0, concat_axis=2, tiled=...  11.9 us
    all_to_all x1, waiting for transfers between devices, shards(): lax.all_to_all(latents, 'frame', split_axis=2, concat_axis=0, tiled=True)  10.3 us
    dot_general x17, matrix products, conv_taps(): jnp.dot(window, weights[3 * row_off + col_off], preferred_element_type=jn...  8.18 us
    ppermute x2, starting transfers between devices, extended(): before = lax.ppermute(last, axis, up)  6.97 us
    all_to_all x1, waiting for transfers between devices, shards(): lax.all_to_all(keyres, 'frame', split_axis=2, concat_axis=0, tiled=True)  6.21 us
    ppermute x2, waiting for transfers between devices, extended(): after = lax.ppermute(initial, axis, down)  5.73 us
    sub x1, matrix products, shards(): weights_soft = jax.nn.softmax(scores, axis=-1).astype(jnp.bfloat16)  5.4 us
    unnamed x27, local copies, waits for them, and re-layouts  5.37 us
  transfers between devices with their start and end apart: 6, of which 5 were waited for; matrix products, arithmetic and copies ran while one was open for 3% of the time, Pallas kernels for 0%

commit v1 on v0

v1 whole, which is shorter than its diff:
```python
import functools
import math

import jax
import jax.numpy as jnp
from jax import lax
from jax.experimental import pallas as pl
from jax.experimental.pallas import tpu as pltpu
from jax.sharding import PartitionSpec as P

HEADS = 8
EPS = 1e-05
BF = jnp.bfloat16
F32 = jnp.float32
LOW = -1e30
LANES = 128
MIB = 1 << 20


def kernel_call(body, outs, cost, limit, scratch=(), smem=0, vmem=0, hbm=0, name=None):
    spaces = [pltpu.SMEM] * smem + [pltpu.VMEM] * vmem + [pl.ANY] * hbm
    return pl.pallas_call(
        body,
        out_shape=outs,
        in_specs=[pl.BlockSpec(memory_space=s) for s in spaces],
        out_specs=jax.tree.map(lambda _: pl.BlockSpec(memory_space=pltpu.VMEM), outs),
        scratch_shapes=list(scratch),
        compiler_params=pltpu.CompilerParams(vmem_limit_bytes=limit * MIB),
        cost_estimate=pl.CostEstimate(flops=cost[0], bytes_accessed=cost[1], transcendentals=0),
        name=name,
    )


def dot(a, b):
    return jnp.dot(a, b, preferred_element_type=F32)


def normalized(x, gain):
    centered = x - jnp.mean(x, axis=-1, keepdims=True)
    variance = jnp.mean(centered * centered, axis=-1, keepdims=True)
    return centered * lax.rsqrt(variance + EPS) * gain


def silu(x):
    return x * jax.nn.sigmoid(x)


def lane_pad(x):
    extra = -x.shape[-1] % LANES
    if not extra:
        return x
    return jnp.concatenate([x, jnp.zeros(x.shape[:-1] + (extra,), x.dtype)], axis=-1)


def conv_rows(rows, w_ref, cols):
    count, channels = rows[1].shape
    taps = jnp.concatenate(
        [
            jnp.concatenate([lane_pad(w_ref[3 * r + c]) for c in range(3)], axis=-1)
            for r in range(3)
        ],
        axis=0,
    )
    wide = taps.shape[1] // 3
    full = dot(jnp.concatenate(rows, axis=-1), taps)
    left, mid, right = [full[:, c * wide : c * wide + channels] for c in range(3)]
    col = lax.broadcasted_iota(jnp.int32, (count, 1), 0) % cols
    left = jnp.where(col == 0, 0.0, pltpu.roll(left, 1, 0))
    right = jnp.where(col == cols - 1, 0.0, pltpu.roll(right, count - 1, 0))
    return left + mid + right


def partner(me, k, size):
    return me ^ k if size & (size - 1) == 0 else lax.rem(me + k, size)


def source(me, k, size):
    return me ^ k if size & (size - 1) == 0 else lax.rem(me + size - k, size)


def swap(x, axis, k):
    size = lax.axis_size(axis)
    if size & (size - 1) == 0:
        pairs = [(i, i ^ k) for i in range(size)]
    else:
        pairs = [(i, (i + k) % size) for i in range(size)]
    return lax.ppermute(x, axis, pairs)


def pairing(x, axis, odd):
    size = lax.axis_size(axis)
    pairs = []
    for i in range(1 if odd else 0, size - 1, 2):
        pairs += [(i, i + 1), (i + 1, i)]
    if not pairs:
        return jnp.zeros_like(x)
    return lax.ppermute(x, axis, pairs)


def parity_of():
    return lax.rem(lax.axis_index("row"), 2)


def window(me, k, n, width):
    if n == 1:
        return pl.ds(0, width)
    return pl.ds(pl.multiple_of(me * width, width), width)


def cut_body(n, cond_ref, lat_ref, ea_ref, eb_ref, *refs):
    outs, sems = refs[:n], refs[n]
    me, parity = lax.axis_index("frame"), parity_of()
    last = cond_ref.shape[1] - 1
    width = lat_ref.shape[2] // n
    copies = [
        pltpu.make_async_copy(cond_ref.at[:, last * (1 - parity)], ea_ref, sems.at[0]),
        pltpu.make_async_copy(cond_ref.at[:, last * parity], eb_ref, sems.at[1]),
    ]
    for k in range(n):
        cut = window(partner(me, k, n), k, n, width)
        copies.append(pltpu.make_async_copy(lat_ref.at[:, :, cut, :], outs[k], sems.at[2 + k]))
    for copy in copies:
        copy.start()
    for copy in copies:
        copy.wait()


def encoder_body(n, cond_ref, ha_ref, hb_ref, w_ref, zero_ref, *refs):
    outs, res, edge = refs[:n], refs[n], refs[n + 1]
    slots, nrows, cols, channels = cond_ref.shape
    parity = parity_of()
    edge[1 - parity] = ha_ref[...]
    edge[parity] = hb_ref[...]
    rows = [edge[0]] + [cond_ref[:, r] for r in range(nrows)] + [edge[1]]
    rows = [r.reshape(slots * cols, channels) for r in rows]
    for r in range(nrows):
        feat = silu(conv_rows(rows[r : r + 3], w_ref, cols)).astype(BF)
        res[:, r] = dot(feat, zero_ref[...]).astype(BF).reshape(slots, cols, channels)
    for k in range(n):
        me = partner(lax.axis_index("frame"), k, n) if n > 1 else 0
        outs[k][...] = res[:, :, window(me, k, n, cols // n), :]


def gathered(ref, rows):
    return jnp.concatenate([ref[t, rows, :] for t in range(ref.shape[0])], axis=-1)


def attention_body(n, kf_ref, prop_ref, *refs):
    lat = refs[:n]
    res = refs[n : 2 * n]
    gain_ref, wq_ref, wk_ref, wv_ref, wo_ref = refs[2 * n : 2 * n + 5]
    outs = refs[2 * n + 5 : 3 * n + 5]
    keyres, hid, tok, qs, ks, vs, ms = refs[3 * n + 5 :]
    frames_dev, pix, channels = lat[0].shape
    slots = res[0].shape[0]
    frames = frames_dev * n
    head_dim = channels // HEADS
    me = lax.axis_index("frame")
    for k in range(n):
        first = source(me, k, n) * slots
        for j in range(slots):
            keyres[first + j] = res[k][j]
    half = lax.broadcasted_iota(jnp.int32, (1, channels), 1)
    freq = jnp.exp((half // 2).astype(F32) * (-2.0 * math.log(10000.0) / channels))
    for k in range(n):
        base = source(me, k, n) * frames_dev
        rows = lax.broadcasted_iota(jnp.int32, (frames_dev, channels), 0) + base
        angle = rows.astype(F32) * freq
        code = jnp.where(half % 2 == 0, jnp.sin(angle), jnp.cos(angle))
        for j in range(frames_dev):
            frame = base + j
            slot = prop_ref[frame]
            gap = jnp.abs(frame - kf_ref[slot]).astype(F32)
            reach = jnp.exp(jnp.full((1, channels), -gap / (2 * frames_dev), F32))
            value = lat[k][j].astype(F32) + reach * keyres[slot].astype(F32)
            hidden = value.astype(BF).astype(F32)
            at = k * frames_dev + j
            hid[at] = hidden
            normed = lane_pad(normalized(hidden, gain_ref[...][None]) + code[j : j + 1])
            for t in range(tok.shape[0]):
                tok[t, pl.ds(at * pix, pix), :] = normed[:, t * LANES : (t + 1) * LANES]
    for p in range(0, pix, 2):
        pair = [gathered(tok, pl.ds(p + i, frames, stride=pix)) for i in range(2)]
        x = jnp.concatenate(pair, axis=0)[:, :channels].astype(BF)
        qs[pl.ds(p * frames, 2 * frames), :] = x
    x = qs[...]
    ks[...] = dot(x, wk_ref[...]).astype(BF)
    vs[...] = dot(x, wv_ref[...]).astype(BF)
    qs[...] = dot(x, wq_ref[...]).astype(BF)
    group = max(d for d in range(1, pix + 1) if pix % d == 0 and (d == 1 or d * frames <= LANES))
    tokens = frames * group
    lane = lax.broadcasted_iota(jnp.int32, (1, channels), 1)
    same = (lax.broadcasted_iota(jnp.int32, (tokens, tokens), 0) // frames) == (
        lax.broadcasted_iota(jnp.int32, (tokens, tokens), 1) // frames
    )
    scale = math.log2(math.e) / math.sqrt(head_dim)
    for g in range(pix // group):
        at = pl.ds(g * tokens, tokens)
        q, kk, v = qs[at, :], ks[at, :], vs[at, :]
        tiles = [None] * (-(-channels // LANES))
        for h in range(HEADS):
            low, high = h * head_dim, (h + 1) * head_dim
            a = low // LANES * LANES
            b = min(-(-high // LANES) * LANES, channels)
            inside = (lane[:, a:b] >= low) & (lane[:, a:b] < high)
            kh = jnp.where(inside, kk[:, a:b], 0)
            vh = jnp.where(inside, v[:, a:b], 0)
            s = lax.dot_general(q[:, a:b], kh, (((1,), (1,)), ((), ())), preferred_element_type=F32)
            if group > 1:
                s = jnp.where(same, s, LOW)
            p = jnp.exp2((s - jnp.max(s, axis=-1, keepdims=True)) * scale)
            p = (p * (1.0 / jnp.sum(p, axis=-1, keepdims=True))).astype(BF)
            o = dot(p, vh)
            for t in range(a // LANES, -(-b // LANES)):
                piece = o[:, t * LANES - a : min((t + 1) * LANES, b) - a]
                tiles[t] = piece if tiles[t] is None else tiles[t] + piece
        ms[at, :] = jnp.concatenate(tiles, axis=-1).astype(BF)
    projected = lane_pad(dot(ms[...], wo_ref[...]))
    for t in range(tok.shape[0]):
        tok[t] = projected[:, t * LANES : (t + 1) * LANES]
    for k in range(n):
        for j in range(frames_dev):
            at = k * frames_dev + j
            mixed = gathered(tok, pl.ds(at, pix, stride=frames))[:, :channels]
            outs[k][j] = (hid[at] + mixed).astype(BF)


def activation_body(n, *refs):
    pieces = refs[:n]
    gain_ref, att_ref, act_ref, ea_ref, eb_ref = refs[n:]
    frames_dev, nrows, width, channels = pieces[0].shape
    parity = parity_of()
    for k in range(n):
        me = source(lax.axis_index("frame"), k, n) if n > 1 else 0
        at = window(me, k, n, width)
        piece = pieces[k][...]
        att_ref[:, :, at, :] = piece
        act = silu(normalized(piece.astype(F32), gain_ref[...].reshape(1, 1, 1, channels)))
        act_ref[:, :, at, :] = act.astype(BF)
    ea_ref[...] = act_ref[:, (nrows - 1) * (1 - parity)]
    eb_ref[...] = act_ref[:, (nrows - 1) * parity]


def block_body(att_ref, act_ref, ha_ref, hb_ref, w_ref, out_ref, edge):
    frames_dev, nrows, cols, channels = act_ref.shape
    parity = parity_of()
    edge[1 - parity] = ha_ref[...]
    edge[parity] = hb_ref[...]
    rows = [edge[0]] + [act_ref[:, r] for r in range(nrows)] + [edge[1]]
    rows = [r.reshape(frames_dev * cols, channels) for r in rows]
    for r in range(nrows):
        conv = conv_rows(rows[r : r + 3], w_ref, cols).reshape(frames_dev, cols, channels)
        out_ref[:, r] = (att_ref[:, r].astype(F32) + conv).astype(BF)


def shards(
    latents,
    condition,
    key_frames,
    propagate,
    encoder_conv,
    zero_conv,
    attention_gain,
    query_weight,
    key_weight,
    value_weight,
    output_weight,
    conv_gain,
    block_conv,
):
    frames_dev, nrows, cols, channels = latents.shape
    slots = condition.shape[0]
    n = lax.axis_size("frame")
    width = cols // n
    frames, pix = frames_dev * n, nrows * width
    me, parity = lax.axis_index("frame"), parity_of()
    sds = jax.ShapeDtypeStruct
    aligned = width % 16 == 0
    parts = n if aligned else 1
    order = [source(me, k, n) for k in range(n)]

    def cut(x, k):
        start = partner(me, k, n) * width
        return lax.dynamic_slice_in_dim(x, start, width, axis=2)

    def flat(x):
        return x.reshape(x.shape[0], pix, channels)

    if aligned:
        edge = sds((slots, cols, channels), BF)
        cond_a, cond_b, *lat = kernel_call(
            functools.partial(cut_body, n),
            [edge, edge] + [sds((frames_dev, nrows, width, channels), BF)] * n,
            (0, 2 * MIB),
            6,
            [pltpu.SemaphoreType.DMA((n + 2,))],
            hbm=2,
            name="cut",
        )(condition, latents)
    else:
        last = nrows - 1
        cond_a = lax.dynamic_index_in_dim(condition, last * (1 - parity), 1, keepdims=False)
        cond_b = lax.dynamic_index_in_dim(condition, last * parity, 1, keepdims=False)
        lat = [cut(latents, k) for k in range(n)]
    halo_a = pairing(cond_a, "row", False)
    halo_b = pairing(cond_b, "row", True)
    lat = [lat[0]] + [swap(lat[k], "frame", k) for k in range(1, n)]
    res = kernel_call(
        functools.partial(encoder_body, parts),
        [sds((slots, nrows, cols // parts, channels), BF)] * parts,
        (2 * slots * nrows * cols * channels * channels * 10, 4 * MIB),
        20,
        [
            pltpu.VMEM((slots, nrows, cols, channels), BF),
            pltpu.VMEM((2, slots, cols, channels), BF),
        ],
        vmem=5,
        name="encoder",
    )(condition, halo_a, halo_b, encoder_conv, zero_conv)
    if not aligned:
        res = [cut(res[0], k) for k in range(n)]
    res = [res[0]] + [swap(res[k], "frame", k) for k in range(1, n)]
    tokens = pltpu.VMEM((frames * pix, channels), BF)
    att = kernel_call(
        functools.partial(attention_body, n),
        [sds((frames_dev, pix, channels), BF)] * n,
        (2 * frames * pix * channels * channels * 8, 4 * MIB),
        24,
        [
            pltpu.VMEM((slots * n, pix, channels), BF),
            pltpu.VMEM((frames, pix, channels), F32),
            pltpu.VMEM((-(-channels // LANES), frames * pix, LANES), F32),
            tokens,
            tokens,
            tokens,
            tokens,
        ],
        smem=2,
        vmem=2 * n + 5,
        name="attention",
    )(
        key_frames,
        propagate,
        *map(flat, lat),
        *map(flat, res),
        attention_gain,
        query_weight,
        key_weight,
        value_weight,
        output_weight,
    )
    att = [a.reshape(frames_dev, nrows, width, channels) for a in att]
    att = [att[0]] + [swap(att[k], "frame", k) for k in range(1, n)]
    if not aligned:
        att = jnp.stack(att)[jnp.stack(order)]
        att = [jnp.moveaxis(att, 0, 2).reshape(latents.shape)]
    whole = sds(latents.shape, BF)
    edge = sds((frames_dev, cols, channels), BF)
    attended, activated, edge_a, edge_b = kernel_call(
        functools.partial(activation_body, parts),
        [whole, whole, edge, edge],
        (10 * frames_dev * nrows * cols * channels, 2 * MIB),
        12,
        vmem=parts + 1,
        name="activation",
    )(*att, conv_gain)
    halo_a = pairing(edge_a, "row", False)
    halo_b = pairing(edge_b, "row", True)
    return kernel_call(
        block_body,
        whole,
        (2 * frames_dev * nrows * cols * channels * channels * 9, 4 * MIB),
        24,
        [pltpu.VMEM((2, frames_dev, cols, channels), BF)],
        vmem=5,
        name="block",
    )(attended, activated, halo_a, halo_b, block_conv)


def solution(mesh):
    image = P(("group", "frame"), "row", None, None)
    placed = (image, image, P("group"), P("group")) + (P(),) * 9
    return jax.shard_map(shards, mesh=mesh, in_specs=placed, out_specs=image, check_vma=False)
```

time: 120 us -> 60.9 us (0.51); the launches traced: 118 us -> 60.4 us
  local copies, waits for them, and re-layouts: 32.3 us -> 5.59 us
  matrix products: 22.9 us -> 0 us
  Pallas kernels: 0 us -> 19.8 us
  blocking collectives: 11.9 us -> 0 us
  waiting for transfers between devices: 26.4 us -> 20.3 us
  other arithmetic: 4.6 us -> 0 us
  starting transfers between devices: 19 us -> 14.6 us
    pallas_call x0 -> x5, Pallas kernels: none -> 19.8 us  [the longest x1 14.3 us: shards(): kernel_call(functools.partial(attention_body, n), [sds((frames_dev, pix,...]
    reshape x10 -> x0, local copies, waits for them, and re-layouts: 19.6 us -> none  [the longest x2 5.33 us: shards(): key_proj = jnp.dot(flattened, key_weight, preferred_element_type=jnp.floa...]
    dot_general x24 -> x0, matrix products: 17.5 us -> none  [the longest x17 8.18 us: conv_taps(): jnp.dot(window, weights[3 * row_off + col_off], preferred_element_type=jn...]
    all_to_all x2 -> x0, waiting for transfers between devices: 16.5 us -> none  [the longest x1 10.3 us: shards(): lax.all_to_all(latents, 'frame', split_axis=2, concat_axis=0, tiled=True)]
    all_to_all x1 -> x0, blocking collectives: 11.9 us -> none  [shards(): lax.all_to_all(attended_pix, 'frame', split_axis=0, concat_axis=2, tiled=...]
    ppermute x4 -> x13, waiting for transfers between devices: 9.96 us -> 20.3 us  [the longest x9 11.1 us: swap(): return lax.ppermute(x, axis, pairs)]
    all_to_all x2 -> x0, starting transfers between devices: 7.26 us -> none  [the longest x1 3.67 us: shards(): lax.all_to_all(latents, 'frame', split_axis=2, concat_axis=0, tiled=True)]
    sub x1 -> x0, matrix products: 5.4 us -> none  [shards(): weights_soft = jax.nn.softmax(scores, axis=-1).astype(jnp.bfloat16)]
  transfers between devices with their start and end apart: 6 -> 13, of which waited for: 5 -> 7; matrix products, arithmetic and copies ran while one was open for 3% -> 0% of each run, Pallas kernels for 0% -> 3%
where the time goes in v1:
time: 60.9 us; the launch traced here: 60.4 us
  waiting for transfers between devices  20.3 us (33%)
  Pallas kernels  19.8 us (33%)
  starting transfers between devices  14.6 us (24%)
  local copies, waits for them, and re-layouts  5.59 us (9%)
    pallas_call x1, Pallas kernels, shards(): kernel_call(functools.partial(attention_body, n), [sds((frames_dev, pix,...  14.3 us
    ppermute x9, waiting for transfers between devices, swap(): return lax.ppermute(x, axis, pairs)  11.1 us
    ppermute x4, waiting for transfers between devices, pairing(): return lax.ppermute(x, axis, pairs)  9.18 us
    ppermute x4, starting transfers between devices, pairing(): return lax.ppermute(x, axis, pairs)  8.82 us
    ppermute x9, starting transfers between devices, swap(): return lax.ppermute(x, axis, pairs)  5.76 us
    unnamed x28, local copies, waits for them, and re-layouts  5.59 us
    pallas_call x1, Pallas kernels, shards(): kernel_call(block_body, whole, (2 * frames_dev * nrows * cols * channels...  3.07 us
    pallas_call x1, Pallas kernels, shards(): kernel_call(functools.partial(encoder_body, parts), [sds((slots, nrows, c...  1.54 us
  transfers between devices with their start and end apart: 13, of which 7 were waited for; matrix products, arithmetic and copies ran while one was open for 0% of the time, Pallas kernels for 3%

profile of v1, /device:TPU:8, one launch (start us, length us, event | category | flops | bytes accessed | tf_op | source)
XLA Modules:
  0.0 60.4 jit_solution(15592968678977029565)
XLA Ops:
  0.0 1.0 %copy-done.1 = bf16[3,2,64,320]{3,2,1,0:T(8,128)(2,1)S(1)} copy-done((bf16[3,2,64,320]{3,2,1,0:T(8,128)(2,1)S(1)}, bf16[3,2,64,320]{3,2,1,0:T(8,128)(2,1)}, u32[]{:S(2)}) %copy-start.1) | copy-done | bytes 245784
  1.0 1.1 %copy-done.3 = bf16[6,2,64,320]{3,2,1,0:T(8,128)(2,1)S(1)} copy-done((bf16[6,2,64,320]{3,2,1,0:T(8,128)(2,1)S(1)}, bf16[6,2,64,320]{3,2,1,0:T(8,128)(2,1)}, u32[]{:S(2)}) %copy-start.3) | copy-done | bytes 491544
  2.1 0.3 cut.1
  2.4 0.1 collective-permute-start.3
  2.4 5.0 %collective-permute-start.4 = (bf16[3,64,320]{2,1,0:T(8,128)(2,1)S(1)}, bf16[3,64,320]{2,1,0:T(8,128)(2,1)S(1)}, u32[]{:S(2)}, u32[]{:S(2)}) collective-permute-start(bf16[3,64,320]{2,1,0:T(8,128)(2,1)S(1)} %get-tuple-element.28), channel_id=1, source_target_pairs={{1,2},{2,1},{5,6},{6,5},{9,10},{10,9},{13,14},{14,13},{17,18},{18,... | collective-permute-start | bytes 368648 | tf_op jit(solution)/shard_map/ppermute | solution.py:97
  7.5 0.1 collective-permute-start
  7.6 1.6 %collective-permute-start.1 = (bf16[6,2,16,320]{3,2,1,0:T(8,128)(2,1)S(1)}, bf16[6,2,16,320]{3,2,1,0:T(8,128)(2,1)S(1)}, u32[]{:S(2)}, u32[]{:S(2)}) collective-permute-start(bf16[6,2,16,320]{3,2,1,0:T(8,128)(2,1)S(1)} %get-tuple-element.25), channel_id=1, source_target_pairs={{0,8},{4,12},{8,0},{12,4},{1,9},{5,13},{9,1},{13,5},{2,10},{6,14},... | collective-permute-start | bytes 368648 | tf_op jit(solution)/shard_map/ppermute | solution.py:87
  9.2 0.3 collective-permute-start.2
  9.4 1.6 %collective-permute-done.4.hb_ref = bf16[3,64,320]{2,1,0:T(8,128)(2,1)S(1)} collective-permute-done((bf16[3,64,320]{2,1,0:T(8,128)(2,1)S(1)}, bf16[3,64,320]{2,1,0:T(8,128)(2,1)S(1)}, u32[]{:S(2)}, u32[]{:S(2)}) %collective-permute-start.4) | collective-permute-done | bytes 122912 | tf_op jit(solution)/shard_map/ppermute | solution.py:97
  11.0 1.6 %copy-done = bf16[9,320,320]{2,1,0:T(8,128)(2,1)S(1)} copy-done((bf16[9,320,320]{2,1,0:T(8,128)(2,1)S(1)}, bf16[9,320,320]{2,1,0:T(8,128)(2,1)}, u32[]{:S(2)}) %copy-start) | copy-done | bytes 1843224
  12.7 1.0 %copy-done.2 = bf16[3,2,64,320]{3,2,1,0:T(8,128)(2,1)S(1)} copy-done((bf16[3,2,64,320]{3,2,1,0:T(8,128)(2,1)S(1)}, bf16[3,2,64,320]{3,2,1,0:T(8,128)(2,1)}, u32[]{:S(2)}) %copy-start.2) | copy-done | bytes 245784
  13.6 0.9 %copy-done.4 = bf16[320,320]{1,0:T(8,128)(2,1)S(1)} copy-done((bf16[320,320]{1,0:T(8,128)(2,1)S(1)}, bf16[320,320]{1,0:T(8,128)(2,1)}, u32[]{:S(2)}) %copy-start.4) | copy-done | bytes 204824
  14.6 1.5 %encoder.1 = (bf16[3,2,16,320]{3,2,1,0:T(8,128)(2,1)S(1)}, bf16[3,2,16,320]{3,2,1,0:T(8,128)(2,1)S(1)}, bf16[3,2,16,320]{3,2,1,0:T(8,128)(2,1)S(1)}, bf16[3,2,16,320]{3,2,1,0:T(8,128)(2,1)S(1)}) custom-call(bf16[3,2,64,320]{3,2,1,0:T(8,128)(2,1)S(1)} %copy-done.2, bf16[3,64,320]{2,1,0:T(8,128)(2,1)S(1)} %collective-permute-done.3.ha_ref, ...), custom_call_target="tpu_custom_call" | custom-call | flops 786432000 | bytes 4194304 | tf_op jit(solution)/shard_map/encoder/pallas_call | solution.py:308
  16.1 0.1 collective-permute-start.5
  16.2 1.6 %collective-permute-start.6 = (bf16[3,2,16,320]{3,2,1,0:T(8,128)(2,1)S(1)}, bf16[3,2,16,320]{3,2,1,0:T(8,128)(2,1)S(1)}, u32[]{:S(2)}, u32[]{:S(2)}) collective-permute-start(bf16[3,2,16,320]{3,2,1,0:T(8,128)(2,1)S(1)} %get-tuple-element.31), channel_id=1, source_target_pairs={{0,8},{4,12},{8,0},{12,4},{1,9},{5,13},{9,1},{13,5},{2,10},{6,14},... | collective-permute-start | bytes 184328 | tf_op jit(solution)/shard_map/ppermute | solution.py:87
  17.8 0.3 collective-permute-start.7
  18.1 2.9 %collective-permute-done.6 = bf16[3,2,16,320]{3,2,1,0:T(8,128)(2,1)S(1)} collective-permute-done((bf16[3,2,16,320]{3,2,1,0:T(8,128)(2,1)S(1)}, bf16[3,2,16,320]{3,2,1,0:T(8,128)(2,1)S(1)}, u32[]{:S(2)}, u32[]{:S(2)}) %collective-permute-start.6) | collective-permute-done | bytes 61472 | tf_op jit(solution)/shard_map/ppermute | solution.py:87
  21.0 1.3 %collective-permute-done.7 = bf16[3,2,16,320]{3,2,1,0:T(8,128)(2,1)S(1)} collective-permute-done((bf16[3,2,16,320]{3,2,1,0:T(8,128)(2,1)S(1)}, bf16[3,2,16,320]{3,2,1,0:T(8,128)(2,1)S(1)}, u32[]{:S(2)}, u32[]{:S(2)}) %collective-permute-start.7) | collective-permute-done | bytes 61472 | tf_op jit(solution)/shard_map/ppermute | solution.py:87
  22.3 0.0 copy-start.5
  22.3 0.0 copy-start.6
  22.3 14.3 %attention.1 = (bf16[6,32,320]{2,1,0:T(8,128)(2,1)S(1)}, bf16[6,32,320]{2,1,0:T(8,128)(2,1)S(1)}, bf16[6,32,320]{2,1,0:T(8,128)(2,1)S(1)}, bf16[6,32,320]{2,1,0:T(8,128)(2,1)S(1)}) custom-call(s32[12]{0:T(128)S(1)} %copy-done.12, s32[24]{0:T(128)S(1)} %copy-done.13, bf16[6,32,320]{2,1,0:T(8,128)(2,1)S(1)} %bitcast.13, bf16[6,32,320]{2,1,0:T(8,128)(2,1)S(1)} %bitcast.14, ...), custom_call_target="tpu_custom_call" | custom-call | flops 1258291200 | bytes 4194304 | tf_op jit(solution)/shard_map/attention/pallas_call | solution.py:324
  36.5 0.2 collective-permute-start.8
  36.7 1.5 %collective-permute-start.9 = (bf16[6,2,16,320]{3,2,1,0:T(8,128)(2,1)S(1)}, bf16[6,2,16,320]{3,2,1,0:T(8,128)(2,1)S(1)}, u32[]{:S(2)}, u32[]{:S(2)}) collective-permute-start(bf16[6,2,16,320]{3,2,1,0:T(8,128)(2,1)S(1)} %bitcast.18), channel_id=1, source_target_pairs={{0,8},{4,12},{8,0},{12,4},{1,9},{5,13},{9,1},{13,5},{2,10},{6,14},... | collective-permute-start | bytes 368648 | tf_op jit(solution)/shard_map/ppermute | solution.py:87
  38.2 0.3 collective-permute-start.10
  38.5 5.0 %collective-permute-done.9.refs_2_ = bf16[6,2,16,320]{3,2,1,0:T(8,128)(2,1)S(1)} collective-permute-done((bf16[6,2,16,320]{3,2,1,0:T(8,128)(2,1)S(1)}, bf16[6,2,16,320]{3,2,1,0:T(8,128)(2,1)S(1)}, u32[]{:S(2)}, u32[]{:S(2)}) %collective-permute-start.9) | collective-permute-done | bytes 122912 | tf_op jit(solution)/shard_map/ppermute | solution.py:87
  43.4 2.0 %collective-permute-done.10.refs_3_ = bf16[6,2,16,320]{3,2,1,0:T(8,128)(2,1)S(1)} collective-permute-done((bf16[6,2,16,320]{3,2,1,0:T(8,128)(2,1)S(1)}, bf16[6,2,16,320]{3,2,1,0:T(8,128)(2,1)S(1)}, u32[]{:S(2)}, u32[]{:S(2)}) %collective-permute-start.10) | collective-permute-done | bytes 122912 | tf_op jit(solution)/shard_map/ppermute | solution.py:87
  45.5 0.6 %activation.1 = (bf16[6,2,64,320]{3,2,1,0:T(8,128)(2,1)S(1)}, bf16[6,2,64,320]{3,2,1,0:T(8,128)(2,1)S(1)}, bf16[6,64,320]{2,1,0:T(8,128)(2,1)S(1)}, bf16[6,64,320]{2,1,0:T(8,128)(2,1)S(1)}) custom-call(bf16[6,2,16,320]{3,2,1,0:T(8,128)(2,1)S(1)} %bitcast.12, bf16[6,2,16,320]{3,2,1,0:T(8,128)(2,1)S(1)} %collective-permute-done.8.refs_1_, ...), custom_call_target="tpu_custom_call" | custom-call | flops 2457600 | bytes 2097152 | tf_op jit(solution)/shard_map/activation/pallas_call | solution.py:359
  46.1 0.1 collective-permute-start.11
  46.2 3.6 %collective-permute-start.12 = (bf16[6,64,320]{2,1,0:T(8,128)(2,1)S(1)}, bf16[6,64,320]{2,1,0:T(8,128)(2,1)S(1)}, u32[]{:S(2)}, u32[]{:S(2)}) collective-permute-start(bf16[6,64,320]{2,1,0:T(8,128)(2,1)S(1)} %get-tuple-element.40), channel_id=1, source_target_pairs={{1,2},{2,1},{5,6},{6,5},{9,10},{10,9},{13,14},{14,13},{17,18},{18,... | collective-permute-start | bytes 737288 | tf_op jit(solution)/shard_map/ppermute | solution.py:97
  49.8 5.6 %collective-permute-done.11.ha_ref = bf16[6,64,320]{2,1,0:T(8,128)(2,1)S(1)} collective-permute-done((bf16[6,64,320]{2,1,0:T(8,128)(2,1)S(1)}, bf16[6,64,320]{2,1,0:T(8,128)(2,1)S(1)}, u32[]{:S(2)}, u32[]{:S(2)}) %collective-permute-start.11) | collective-permute-done | bytes 245792 | tf_op jit(solution)/shard_map/ppermute | solution.py:97
  55.5 1.9 %collective-permute-done.12.hb_ref = bf16[6,64,320]{2,1,0:T(8,128)(2,1)S(1)} collective-permute-done((bf16[6,64,320]{2,1,0:T(8,128)(2,1)S(1)}, bf16[6,64,320]{2,1,0:T(8,128)(2,1)S(1)}, u32[]{:S(2)}, u32[]{:S(2)}) %collective-permute-start.12) | collective-permute-done | bytes 245792 | tf_op jit(solution)/shard_map/ppermute | solution.py:97
  57.4 3.1 %block.1 = bf16[6,2,64,320]{3,2,1,0:T(8,128)(2,1)} custom-call(bf16[6,2,64,320]{3,2,1,0:T(8,128)(2,1)S(1)} %get-tuple-element.37.att_ref, bf16[6,2,64,320]{3,2,1,0:T(8,128)(2,1)S(1)} %get-tuple-element.38.act_ref, bf16[6,64,320]{2,1,0:T(8,128)(2,1)S(1)} %collective-permute-done.11.ha_ref, bf16[6,64,320]{2,1,0:T(8,128)(2,1)S(1)} %collective-permute-done.12.hb_ref, ...), custom_call_target="tpu_custom_call" | custom-call | flops 1415577600 | bytes 4194304 | tf_op jit(solution)/shard_map/block/pallas_call | solution.py:369
  (27 shorter events, 0.1 us)
Async XLA Ops:
  0.0 1.0 %copy-start.1 = (bf16[3,2,64,320]{3,2,1,0:T(8,128)(2,1)S(1)}, bf16[3,2,64,320]{3,2,1,0:T(8,128)(2,1)}, u32[]{:S(2)}) copy-start(bf16[3,2,64,320]{3,2,1,0:T(8,128)(2,1)} %cond_ref.3) | copy-start | bytes 737284
  1.0 1.1 %copy-start.3 = (bf16[6,2,64,320]{3,2,1,0:T(8,128)(2,1)S(1)}, bf16[6,2,64,320]{3,2,1,0:T(8,128)(2,1)}, u32[]{:S(2)}) copy-start(bf16[6,2,64,320]{3,2,1,0:T(8,128)(2,1)} %lat_ref.1) | copy-start | bytes 1474564
  2.0 20.2 %copy-start.7 = (bf16[320,320]{1,0:T(8,128)(2,1)S(1)}, bf16[320,320]{1,0:T(8,128)(2,1)}, u32[]{:S(2)}) copy-start(bf16[320,320]{1,0:T(8,128)(2,1)} %refs_9_.1) | copy-start | bytes 614404
  2.0 20.2 %copy-start.8 = (bf16[320,320]{1,0:T(8,128)(2,1)S(1)}, bf16[320,320]{1,0:T(8,128)(2,1)}, u32[]{:S(2)}) copy-start(bf16[320,320]{1,0:T(8,128)(2,1)} %refs_10_.1) | copy-start | bytes 614404
  2.0 20.2 %copy-start.9 = (bf16[320,320]{1,0:T(8,128)(2,1)S(1)}, bf16[320,320]{1,0:T(8,128)(2,1)}, u32[]{:S(2)}) copy-start(bf16[320,320]{1,0:T(8,128)(2,1)} %refs_11_.1) | copy-start | bytes 614404
  2.0 20.2 %copy-start.11 = (f32[320]{0:T(512)S(1)}, f32[320]{0:T(512)}, u32[]{:S(2)}) copy-start(f32[320]{0:T(512)} %refs_8_.1) | copy-start | bytes 3844
  2.0 20.2 %copy-start.12 = (s32[12]{0:T(128)S(1)}, s32[12]{0:T(128)}, u32[]{:S(2)}) copy-start(s32[12]{0:T(128)} %kf_ref.1) | copy-start | bytes 148
  2.0 20.2 %copy-start.13 = (s32[24]{0:T(128)S(1)}, s32[24]{0:T(128)}, u32[]{:S(2)}) copy-start(s32[24]{0:T(128)} %prop_ref.1) | copy-start | bytes 292
  2.4 7.1 %collective-permute-start.3 = (bf16[3,64,320]{2,1,0:T(8,128)(2,1)S(1)}, bf16[3,64,320]{2,1,0:T(8,128)(2,1)S(1)}, u32[]{:S(2)}, u32[]{:S(2)}) collective-permute-start(bf16[3,64,320]{2,1,0:T(8,128)(2,1)S(1)} %get-tuple-element.27), channel_id=1, source_target_pairs={{0,1},{1,0},{2,3},{3,2},{4,5},{5,4},{6,7},{7,6},{8,9},{9,8},{10,11... | collective-permute-start | bytes 368648 | tf_op jit(solution)/shard_map/ppermute | solution.py:97
  2.4 8.6 %collective-permute-start.4 = (bf16[3,64,320]{2,1,0:T(8,128)(2,1)S(1)}, bf16[3,64,320]{2,1,0:T(8,128)(2,1)S(1)}, u32[]{:S(2)}, u32[]{:S(2)}) collective-permute-start(bf16[3,64,320]{2,1,0:T(8,128)(2,1)S(1)} %get-tuple-element.28), channel_id=1, source_target_pairs={{1,2},{2,1},{5,6},{6,5},{9,10},{10,9},{13,14},{14,13},{17,18},{18,... | collective-permute-start | bytes 368648 | tf_op jit(solution)/shard_map/ppermute | solution.py:97
  7.5 10.3 %collective-permute-start = (bf16[6,2,16,320]{3,2,1,0:T(8,128)(2,1)S(1)}, bf16[6,2,16,320]{3,2,1,0:T(8,128)(2,1)S(1)}, u32[]{:S(2)}, u32[]{:S(2)}) collective-permute-start(bf16[6,2,16,320]{3,2,1,0:T(8,128)(2,1)S(1)} %get-tuple-element.24), channel_id=1, source_target_pairs={{0,4},{4,0},{8,12},{12,8},{1,5},{5,1},{9,13},{13,9},{2,6},{6,2},{1... | collective-permute-start | bytes 368648 | tf_op jit(solution)/shard_map/ppermute | solution.py:87
  7.6 10.5 %collective-permute-start.1 = (bf16[6,2,16,320]{3,2,1,0:T(8,128)(2,1)S(1)}, bf16[6,2,16,320]{3,2,1,0:T(8,128)(2,1)S(1)}, u32[]{:S(2)}, u32[]{:S(2)}) collective-permute-start(bf16[6,2,16,320]{3,2,1,0:T(8,128)(2,1)S(1)} %get-tuple-element.25), channel_id=1, source_target_pairs={{0,8},{4,12},{8,0},{12,4},{1,9},{5,13},{9,1},{13,5},{2,10},{6,14},... | collective-permute-start | bytes 368648 | tf_op jit(solution)/shard_map/ppermute | solution.py:87
  9.2 8.9 %collective-permute-start.2 = (bf16[6,2,16,320]{3,2,1,0:T(8,128)(2,1)S(1)}, bf16[6,2,16,320]{3,2,1,0:T(8,128)(2,1)S(1)}, u32[]{:S(2)}, u32[]{:S(2)}) collective-permute-start(bf16[6,2,16,320]{3,2,1,0:T(8,128)(2,1)S(1)} %get-tuple-element.26), channel_id=1, source_target_pairs={{0,12},{4,8},{8,4},{12,0},{1,13},{5,9},{9,5},{13,1},{2,14},{6,10},... | collective-permute-start | bytes 368648 | tf_op jit(solution)/shard_map/ppermute | solution.py:87
  11.0 1.6 %copy-start = (bf16[9,320,320]{2,1,0:T(8,128)(2,1)S(1)}, bf16[9,320,320]{2,1,0:T(8,128)(2,1)}, u32[]{:S(2)}) copy-start(bf16[9,320,320]{2,1,0:T(8,128)(2,1)} %w_ref.2) | copy-start | bytes 5529604
  12.7 1.0 %copy-start.2 = (bf16[3,2,64,320]{3,2,1,0:T(8,128)(2,1)S(1)}, bf16[3,2,64,320]{3,2,1,0:T(8,128)(2,1)}, u32[]{:S(2)}) copy-start(bf16[3,2,64,320]{3,2,1,0:T(8,128)(2,1)} %cond_ref.3) | copy-start | bytes 737284
  13.6 0.9 %copy-start.4 = (bf16[320,320]{1,0:T(8,128)(2,1)S(1)}, bf16[320,320]{1,0:T(8,128)(2,1)}, u32[]{:S(2)}) copy-start(bf16[320,320]{1,0:T(8,128)(2,1)} %zero_ref.1) | copy-start | bytes 614404
  14.6 7.7 %copy-start.10 = (bf16[320,320]{1,0:T(8,128)(2,1)S(1)}, bf16[320,320]{1,0:T(8,128)(2,1)}, u32[]{:S(2)}) copy-start(bf16[320,320]{1,0:T(8,128)(2,1)} %refs_12_.1) | copy-start | bytes 614404
  16.1 1.9 %collective-permute-start.5 = (bf16[3,2,16,320]{3,2,1,0:T(8,128)(2,1)S(1)}, bf16[3,2,16,320]{3,2,1,0:T(8,128)(2,1)S(1)}, u32[]{:S(2)}, u32[]{:S(2)}) collective-permute-start(bf16[3,2,16,320]{3,2,1,0:T(8,128)(2,1)S(1)} %get-tuple-element.30), channel_id=1, source_target_pairs={{0,4},{4,0},{8,12},{12,8},{1,5},{5,1},{9,13},{13,9},{2,6},{6,2},{1... | collective-permute-start | bytes 184328 | tf_op jit(solution)/shard_map/ppermute | solution.py:87
  16.2 4.8 %collective-permute-start.6 = (bf16[3,2,16,320]{3,2,1,0:T(8,128)(2,1)S(1)}, bf16[3,2,16,320]{3,2,1,0:T(8,128)(2,1)S(1)}, u32[]{:S(2)}, u32[]{:S(2)}) collective-permute-start(bf16[3,2,16,320]{3,2,1,0:T(8,128)(2,1)S(1)} %get-tuple-element.31), channel_id=1, source_target_pairs={{0,8},{4,12},{8,0},{12,4},{1,9},{5,13},{9,1},{13,5},{2,10},{6,14},... | collective-permute-start | bytes 184328 | tf_op jit(solution)/shard_map/ppermute | solution.py:87
  17.8 4.4 %collective-permute-start.7 = (bf16[3,2,16,320]{3,2,1,0:T(8,128)(2,1)S(1)}, bf16[3,2,16,320]{3,2,1,0:T(8,128)(2,1)S(1)}, u32[]{:S(2)}, u32[]{:S(2)}) collective-permute-start(bf16[3,2,16,320]{3,2,1,0:T(8,128)(2,1)S(1)} %get-tuple-element.32), channel_id=1, source_target_pairs={{0,12},{4,8},{8,4},{12,0},{1,13},{5,9},{9,5},{13,1},{2,14},{6,10},... | collective-permute-start | bytes 184328 | tf_op jit(solution)/shard_map/ppermute | solution.py:87
  22.3 23.2 %copy-start.5 = (f32[320]{0:T(512)S(1)}, f32[320]{0:T(512)}, u32[]{:S(2)}) copy-start(f32[320]{0:T(512)} %refs_4_.1) | copy-start | bytes 3844
  22.3 35.1 %copy-start.6 = (bf16[9,320,320]{2,1,0:T(8,128)(2,1)S(1)}, bf16[9,320,320]{2,1,0:T(8,128)(2,1)}, u32[]{:S(2)}) copy-start(bf16[9,320,320]{2,1,0:T(8,128)(2,1)} %w_ref.3) | copy-start | bytes 5529604
  36.5 1.9 %collective-permute-start.8 = (bf16[6,2,16,320]{3,2,1,0:T(8,128)(2,1)S(1)}, bf16[6,2,16,320]{3,2,1,0:T(8,128)(2,1)S(1)}, u32[]{:S(2)}, u32[]{:S(2)}) collective-permute-start(bf16[6,2,16,320]{3,2,1,0:T(8,128)(2,1)S(1)} %bitcast.19), channel_id=1, source_target_pairs={{0,4},{4,0},{8,12},{12,8},{1,5},{5,1},{9,13},{13,9},{2,6},{6,2},{1... | collective-permute-start | bytes 368648 | tf_op jit(solution)/shard_map/ppermute | solution.py:87
  36.7 6.7 %collective-permute-start.9 = (bf16[6,2,16,320]{3,2,1,0:T(8,128)(2,1)S(1)}, bf16[6,2,16,320]{3,2,1,0:T(8,128)(2,1)S(1)}, u32[]{:S(2)}, u32[]{:S(2)}) collective-permute-start(bf16[6,2,16,320]{3,2,1,0:T(8,128)(2,1)S(1)} %bitcast.18), channel_id=1, source_target_pairs={{0,8},{4,12},{8,0},{12,4},{1,9},{5,13},{9,1},{13,5},{2,10},{6,14},... | collective-permute-start | bytes 368648 | tf_op jit(solution)/shard_map/ppermute | solution.py:87
  38.2 7.3 %collective-permute-start.10 = (bf16[6,2,16,320]{3,2,1,0:T(8,128)(2,1)S(1)}, bf16[6,2,16,320]{3,2,1,0:T(8,128)(2,1)S(1)}, u32[]{:S(2)}, u32[]{:S(2)}) collective-permute-start(bf16[6,2,16,320]{3,2,1,0:T(8,128)(2,1)S(1)} %bitcast.17), channel_id=1, source_target_pairs={{0,12},{4,8},{8,4},{12,0},{1,13},{5,9},{9,5},{13,1},{2,14},{6,10},... | collective-permute-start | bytes 368648 | tf_op jit(solution)/shard_map/ppermute | solution.py:87
  46.1 9.4 %collective-permute-start.11 = (bf16[6,64,320]{2,1,0:T(8,128)(2,1)S(1)}, bf16[6,64,320]{2,1,0:T(8,128)(2,1)S(1)}, u32[]{:S(2)}, u32[]{:S(2)}) collective-permute-start(bf16[6,64,320]{2,1,0:T(8,128)(2,1)S(1)} %get-tuple-element.39), channel_id=1, source_target_pairs={{0,1},{1,0},{2,3},{3,2},{4,5},{5,4},{6,7},{7,6},{8,9},{9,8},{10,11... | collective-permute-start | bytes 737288 | tf_op jit(solution)/shard_map/ppermute | solution.py:97
  46.2 11.2 %collective-permute-start.12 = (bf16[6,64,320]{2,1,0:T(8,128)(2,1)S(1)}, bf16[6,64,320]{2,1,0:T(8,128)(2,1)S(1)}, u32[]{:S(2)}, u32[]{:S(2)}) collective-permute-start(bf16[6,64,320]{2,1,0:T(8,128)(2,1)S(1)} %get-tuple-element.40), channel_id=1, source_target_pairs={{1,2},{2,1},{5,6},{6,5},{9,10},{10,9},{13,14},{14,13},{17,18},{18,... | collective-permute-start | bytes 737288 | tf_op jit(solution)/shard_map/ppermute | solution.py:97

commit v2 on v1

v2 whole, which is shorter than its diff:
```python
import functools
import math

import jax
import jax.numpy as jnp
from jax import lax
from jax.experimental import pallas as pl
from jax.experimental.pallas import tpu as pltpu
from jax.sharding import PartitionSpec as P

HEADS = 8
EPS = 1e-05
BF = jnp.bfloat16
F32 = jnp.float32
LOW = -1e30
LANES = 128
MIB = 1 << 20


def kernel_call(body, outs, cost, limit, scratch=(), smem=0, vmem=0, hbm=0, name=None):
    spaces = [pltpu.SMEM] * smem + [pltpu.VMEM] * vmem + [pltpu.HBM] * hbm
    return pl.pallas_call(
        body,
        out_shape=outs,
        in_specs=[pl.BlockSpec(memory_space=s) for s in spaces],
        out_specs=jax.tree.map(lambda _: pl.BlockSpec(memory_space=pltpu.VMEM), outs),
        scratch_shapes=list(scratch),
        compiler_params=pltpu.CompilerParams(vmem_limit_bytes=limit * MIB),
        cost_estimate=pl.CostEstimate(flops=cost[0], bytes_accessed=cost[1], transcendentals=0),
        name=name,
    )


def dot(a, b):
    return jnp.dot(a, b, preferred_element_type=F32)


def normalized(x, gain):
    centered = x - jnp.mean(x, axis=-1, keepdims=True)
    variance = jnp.mean(centered * centered, axis=-1, keepdims=True)
    return centered * lax.rsqrt(variance + EPS) * gain


def silu(x):
    return x * jax.nn.sigmoid(x)


def lane_pad(x):
    extra = -x.shape[-1] % LANES
    if not extra:
        return x
    return jnp.concatenate([x, jnp.zeros(x.shape[:-1] + (extra,), x.dtype)], axis=-1)


def taps_of(w_ref, row):
    return jnp.concatenate([lane_pad(w_ref[3 * row + c]) for c in range(3)], axis=-1)


def col_shifts(full, channels, cols):
    count, wide = full.shape[0], full.shape[1] // 3
    left, mid, right = [full[:, c * wide : c * wide + channels] for c in range(3)]
    col = lax.broadcasted_iota(jnp.int32, (count, 1), 0) % cols
    left = jnp.where(col == 0, 0.0, pltpu.roll(left, 1, 0))
    right = jnp.where(col == cols - 1, 0.0, pltpu.roll(right, count - 1, 0))
    return left + mid + right


def conv_own(rows, w_ref, r, cols):
    near = [i for i in (r - 1, r, r + 1) if 0 <= i < len(rows)]
    taps = jnp.concatenate([taps_of(w_ref, i - r + 1) for i in near], axis=0)
    full = dot(jnp.concatenate([rows[i] for i in near], axis=-1), taps)
    return col_shifts(full, rows[0].shape[1], cols)


def conv_edge(halo, w_ref, row, cols):
    return col_shifts(dot(halo, taps_of(w_ref, row)), halo.shape[1], cols)


def positions(frames, channels):
    frame = jnp.arange(frames, dtype=F32)[:, None]
    freq = jnp.exp(jnp.arange(channels // 2, dtype=F32) * (-2.0 * math.log(10000.0) / channels))
    angles = frame * freq
    return jnp.stack([jnp.sin(angles), jnp.cos(angles)], axis=-1).reshape(frames, channels)


def partner(me, k, size):
    return me ^ k if size & (size - 1) == 0 else lax.rem(me + k, size)


def source(me, k, size):
    return me ^ k if size & (size - 1) == 0 else lax.rem(me + size - k, size)


def swap(x, axis, k):
    size = lax.axis_size(axis)
    if size & (size - 1) == 0:
        pairs = [(i, i ^ k) for i in range(size)]
    else:
        pairs = [(i, (i + k) % size) for i in range(size)]
    return lax.ppermute(x, axis, pairs)


def pairing(x, axis, odd):
    size = lax.axis_size(axis)
    pairs = []
    for i in range(1 if odd else 0, size - 1, 2):
        pairs += [(i, i + 1), (i + 1, i)]
    if not pairs:
        return jnp.zeros_like(x)
    return lax.ppermute(x, axis, pairs)


def parity_of():
    return lax.rem(lax.axis_index("row"), 2)


def sided(near, far):
    even = parity_of() == 0
    return jnp.where(even, far, near), jnp.where(even, near, far)


def window(me, k, n, width):
    if n == 1:
        return pl.ds(0, width)
    return pl.ds(pl.multiple_of(me * width, width), width)


def cut_body(n, cond_ref, lat_ref, ea_ref, eb_ref, *refs):
    outs, sems = refs[:n], refs[n]
    me, parity = lax.axis_index("frame"), parity_of()
    last = cond_ref.shape[1] - 1
    width = lat_ref.shape[2] // n
    copies = [
        pltpu.make_async_copy(cond_ref.at[:, last * (1 - parity)], ea_ref, sems.at[0]),
        pltpu.make_async_copy(cond_ref.at[:, last * parity], eb_ref, sems.at[1]),
    ]
    for k in range(n):
        cut = window(partner(me, k, n), k, n, width)
        copies.append(pltpu.make_async_copy(lat_ref.at[:, :, cut, :], outs[k], sems.at[2 + k]))
    for copy in copies:
        copy.start()
    for copy in copies:
        copy.wait()


def encoder_own_body(cond_hbm, w_hbm, zero_hbm, acc_ref, w_ref, zero_ref, cond_ref, sems):
    copies = [
        pltpu.make_async_copy(cond_hbm, cond_ref, sems.at[0]),
        pltpu.make_async_copy(w_hbm, w_ref, sems.at[1]),
        pltpu.make_async_copy(zero_hbm, zero_ref, sems.at[2]),
    ]
    for copy in copies:
        copy.start()
    for copy in copies:
        copy.wait()
    slots, nrows, cols, channels = cond_ref.shape
    rows = [cond_ref[:, r].reshape(slots * cols, channels) for r in range(nrows)]
    for r in range(nrows):
        acc_ref[r] = conv_own(rows, w_ref, r, cols)


def encoder_edge_body(n, acc_ref, ha_ref, hb_ref, w_ref, zero_ref, *refs):
    outs, res = refs[:n], refs[n]
    slots, nrows, cols, channels = res.shape
    edge = sided(ha_ref[...], hb_ref[...])
    for r in range(nrows):
        total = acc_ref[r]
        if r == 0:
            total = total + conv_edge(edge[0].reshape(-1, channels), w_ref, 0, cols)
        if r == nrows - 1:
            total = total + conv_edge(edge[1].reshape(-1, channels), w_ref, 2, cols)
        feat = silu(total).astype(BF)
        res[:, r] = dot(feat, zero_ref[...]).astype(BF).reshape(slots, cols, channels)
    for k in range(n):
        me = partner(lax.axis_index("frame"), k, n) if n > 1 else 0
        outs[k][...] = res[:, :, window(me, k, n, cols // n), :]


def gathered(ref, rows):
    return jnp.concatenate([ref[t, rows, :] for t in range(ref.shape[0])], axis=-1)


def attention_body(n, kf_ref, prop_ref, *refs):
    lat = refs[:n]
    res = refs[n : 2 * n]
    code_ref, gain_ref, wq_ref, wk_ref, wv_ref, wo_ref = refs[2 * n : 2 * n + 6]
    outs = refs[2 * n + 6 : -9]
    keyres, hid, tok, qs, ks, vs, bias, scores, probs = refs[-9:]
    frames_dev, pix, channels = lat[0].shape
    slots = res[0].shape[0]
    frames = frames_dev * n
    head_dim = channels // HEADS
    me = lax.axis_index("frame")
    for k in range(n):
        first = source(me, k, n) * slots
        for j in range(slots):
            keyres[first + j] = res[k][j]
    for k in range(n):
        home = source(me, k, n)
        code = code_ref[home]
        for j in range(frames_dev):
            frame = home * frames_dev + j
            slot = prop_ref[frame]
            gap = jnp.abs(frame - kf_ref[slot]).astype(F32)
            reach = jnp.exp(jnp.full((1, channels), -gap / (2 * frames_dev), F32))
            value = lat[k][j].astype(F32) + reach * keyres[slot].astype(F32)
            hidden = value.astype(BF).astype(F32)
            at = k * frames_dev + j
            hid[at] = hidden
            normed = lane_pad(normalized(hidden, gain_ref[...][None]) + code[j : j + 1])
            for t in range(tok.shape[0]):
                tok[t, pl.ds(at * pix, pix), :] = normed[:, t * LANES : (t + 1) * LANES]
    for p in range(0, pix, 2):
        pair = [gathered(tok, pl.ds(p + i, frames, stride=pix)) for i in range(2)]
        x = jnp.concatenate(pair, axis=0)[:, :channels].astype(BF)
        qs[pl.ds(p * frames, 2 * frames), :] = x
    weights = [lane_pad(w[...]) for w in (wq_ref, wk_ref, wv_ref)]
    qkv = dot(qs[...], jnp.concatenate(weights, axis=-1))
    wide = qkv.shape[1] // 3
    for i, ref in enumerate((qs, ks, vs)):
        ref[...] = qkv[:, i * wide : i * wide + channels].astype(BF)
    group = max(d for d in range(1, pix + 1) if pix % d == 0 and (d == 1 or d * frames <= LANES))
    tokens = frames * group
    wide = bias.shape[1]
    lane = lax.broadcasted_iota(jnp.int32, (1, channels), 1)
    row_pix = lax.broadcasted_iota(jnp.int32, (tokens, wide), 0) // frames
    col_pix = lax.broadcasted_iota(jnp.int32, (tokens, wide), 1) // frames
    bias[...] = jnp.where(row_pix == col_pix, 0.0, LOW)
    scale = math.log2(math.e) / math.sqrt(head_dim)

    def span(pair):
        low, high = pair * head_dim, (pair + 2) * head_dim
        return low // LANES * LANES, min(-(-high // LANES) * LANES, channels)

    def stacked(x, pair):
        a, b = span(pair)
        fill = jnp.zeros((wide - tokens, b - a), x.dtype)
        rows = []
        for h in (pair, pair + 1):
            inside = (lane[:, a:b] >= h * head_dim) & (lane[:, a:b] < (h + 1) * head_dim)
            rows += [jnp.where(inside, x[:, a:b], 0)] + ([fill] if wide > tokens else [])
        return jnp.concatenate(rows, axis=0)

    def score(g):
        at = pl.ds(g * tokens, tokens)
        q, kk = qs[at, :], ks[at, :]
        for pair in range(0, HEADS, 2):
            a, b = span(pair)
            s = lax.dot_general(
                q[:, a:b],
                stacked(kk, pair),
                (((1,), (1,)), ((), ())),
                preferred_element_type=F32,
            )
            scores[g % 2, :, pair * wide : (pair + 2) * wide] = s

    def weigh(g):
        for h in range(HEADS):
            s = scores[g % 2, :, h * wide : (h + 1) * wide] + bias[...]
            p = jnp.exp2((s - jnp.max(s, axis=-1, keepdims=True)) * scale)
            p = p * (1.0 / jnp.sum(p, axis=-1, keepdims=True))
            probs[g % 2, :, h * wide : (h + 1) * wide] = p.astype(BF)

    def mix(g):
        at = pl.ds(g * tokens, tokens)
        v = vs[at, :]
        tiles = [None] * (-(-channels // LANES))
        for pair in range(0, HEADS, 2):
            a, b = span(pair)
            o = dot(probs[g % 2, :, pair * wide : (pair + 2) * wide], stacked(v, pair))
            for t in range(a // LANES, -(-b // LANES)):
                piece = o[:, t * LANES - a : min((t + 1) * LANES, b) - a]
                tiles[t] = piece if tiles[t] is None else tiles[t] + piece
        vs[at, :] = jnp.concatenate(tiles, axis=-1).astype(BF)

    groups = pix // group
    for step in range(groups + 2):
        if step < groups:
            score(step)
        if 0 <= step - 1 < groups:
            weigh(step - 1)
        if 0 <= step - 2:
            mix(step - 2)
    projected = lane_pad(dot(vs[...], wo_ref[...]))
    for t in range(tok.shape[0]):
        tok[t] = projected[:, t * LANES : (t + 1) * LANES]
    for k in range(n):
        for j in range(frames_dev):
            at = k * frames_dev + j
            mixed = gathered(tok, pl.ds(at, pix, stride=frames))[:, :channels]
            piece = len(outs) // n * j // frames_dev
            row = j - frames_dev * piece // (len(outs) // n)
            outs[piece * n + k][row] = (hid[at] + mixed).astype(BF)


def activation_body(n, *refs):
    pieces = refs[:n]
    gain_ref, att_ref, act_ref, ea_ref, eb_ref = refs[n:]
    frames_dev, nrows, width, channels = pieces[0].shape
    parity = parity_of()
    for k in range(n):
        me = source(lax.axis_index("frame"), k, n) if n > 1 else 0
        at = window(me, k, n, width)
        piece = pieces[k][...]
        att_ref[:, :, at, :] = piece
        act = silu(normalized(piece.astype(F32), gain_ref[...].reshape(1, 1, 1, channels)))
        act_ref[:, :, at, :] = act.astype(BF)
    ea_ref[...] = act_ref[:, (nrows - 1) * (1 - parity)]
    eb_ref[...] = act_ref[:, (nrows - 1) * parity]


def block_own_body(att_ref, act_ref, w_ref, acc_ref):
    count, nrows, cols, channels = act_ref.shape
    rows = [act_ref[:, r].reshape(count * cols, channels) for r in range(nrows)]
    for r in range(nrows):
        conv = conv_own(rows, w_ref, r, cols).reshape(count, cols, channels)
        acc_ref[:, r] = att_ref[:, r].astype(F32) + conv


def block_edge_body(m, *refs):
    accs, near, far = refs[:m], refs[m : 2 * m], refs[2 * m : 3 * m]
    w_ref, out_ref = refs[3 * m :]
    for i in range(m):
        count, nrows, cols, channels = accs[i].shape
        edge = sided(near[i][...], far[i][...])
        for r in range(nrows):
            total = accs[i][:, r]
            for side, at in ((0, 0), (1, nrows - 1)):
                if r == at:
                    conv = conv_edge(edge[side].reshape(-1, channels), w_ref, 2 * side, cols)
                    total = total + conv.reshape(count, cols, channels)
            out_ref[pl.ds(i * count, count), r] = total.astype(BF)


def shards(
    latents,
    condition,
    key_frames,
    propagate,
    encoder_conv,
    zero_conv,
    attention_gain,
    query_weight,
    key_weight,
    value_weight,
    output_weight,
    conv_gain,
    block_conv,
):
    frames_dev, nrows, cols, channels = latents.shape
    slots = condition.shape[0]
    n = lax.axis_size("frame")
    width = cols // n
    frames, pix = frames_dev * n, nrows * width
    me, parity = lax.axis_index("frame"), parity_of()
    sds = jax.ShapeDtypeStruct
    aligned = width % 16 == 0
    parts = n if aligned else 1
    order = [source(me, k, n) for k in range(n)]

    def cut(x, k):
        start = partner(me, k, n) * width
        return lax.dynamic_slice_in_dim(x, start, width, axis=2)

    def flat(x):
        return x.reshape(x.shape[0], pix, channels)

    if aligned:
        edge = sds((slots, cols, channels), BF)
        cond_a, cond_b, *lat = kernel_call(
            functools.partial(cut_body, n),
            [edge, edge] + [sds((frames_dev, nrows, width, channels), BF)] * n,
            (0, 2 * MIB),
            6,
            [pltpu.SemaphoreType.DMA((n + 2,))],
            hbm=2,
            name="cut",
        )(condition, latents)
    else:
        last = nrows - 1
        cond_a = lax.dynamic_index_in_dim(condition, last * (1 - parity), 1, keepdims=False)
        cond_b = lax.dynamic_index_in_dim(condition, last * parity, 1, keepdims=False)
        lat = [cut(latents, k) for k in range(n)]
    halo_a = pairing(cond_a, "row", False)
    halo_b = pairing(cond_b, "row", True)
    lat = [lat[0]] + [swap(lat[k], "frame", k) for k in range(1, n)]
    macs = nrows * cols * channels * channels
    vmem = pltpu.VMEM
    acc, enc_w, zero_w = kernel_call(
        encoder_own_body,
        [
            sds((nrows, slots * cols, channels), F32),
            sds(encoder_conv.shape, BF),
            sds(zero_conv.shape, BF),
        ],
        (12 * slots * macs, 4 * MIB),
        16,
        [vmem(condition.shape, BF), pltpu.SemaphoreType.DMA((3,))],
        hbm=3,
        name="encoder_own",
    )(condition, encoder_conv, zero_conv)
    res = kernel_call(
        functools.partial(encoder_edge_body, parts),
        [sds((slots, nrows, cols // parts, channels), BF)] * parts,
        (8 * slots * macs, 4 * MIB),
        16,
        [vmem(condition.shape, BF)],
        vmem=5,
        name="encoder_edge",
    )(acc, halo_a, halo_b, enc_w, zero_w)
    if not aligned:
        res = [cut(res[0], k) for k in range(n)]
    res = [res[0]] + [swap(res[k], "frame", k) for k in range(1, n)]
    code = positions(frames, channels).reshape(n, frames_dev, channels)
    halves = 2 if frames_dev % 2 == 0 else 1
    share = frames_dev // halves
    tokens = vmem((frames * pix, channels), BF)
    group = max(d for d in range(1, pix + 1) if pix % d == 0 and (d == 1 or d * frames <= LANES))
    wide = -(-group * frames // LANES) * LANES
    pieces = kernel_call(
        functools.partial(attention_body, n),
        [sds((share, pix, channels), BF)] * (halves * n),
        (2 * frames * pix * channels * channels * 8, 4 * MIB),
        24,
        [
            vmem((slots * n, pix, channels), BF),
            vmem((frames, pix, channels), F32),
            vmem((-(-channels // LANES), frames * pix, LANES), F32),
            tokens,
            tokens,
            tokens,
            vmem((group * frames, wide), F32),
            vmem((2, group * frames, HEADS * wide), F32),
            vmem((2, group * frames, HEADS * wide), BF),
        ],
        smem=2,
        vmem=2 * n + 6,
        name="attention",
    )(
        key_frames,
        propagate,
        *map(flat, lat),
        *map(flat, res),
        code,
        attention_gain,
        query_weight,
        key_weight,
        value_weight,
        output_weight,
    )
    shape = (share, nrows, cols, channels)
    accs, near, far = [], [], []
    for i in range(halves):
        att = [p.reshape(share, nrows, width, channels) for p in pieces[i * n : (i + 1) * n]]
        att = [att[0]] + [swap(att[k], "frame", k) for k in range(1, n)]
        if not aligned:
            att = jnp.stack(att)[jnp.stack(order)]
            att = [jnp.moveaxis(att, 0, 2).reshape(shape)]
        edge = sds((share, cols, channels), BF)
        attended, activated, edge_a, edge_b = kernel_call(
            functools.partial(activation_body, parts),
            [sds(shape, BF), sds(shape, BF), edge, edge],
            (10 * share * nrows * cols * channels, 2 * MIB),
            8,
            vmem=parts + 1,
            name="activation",
        )(*att, conv_gain)
        near.append(pairing(edge_a, "row", False))
        far.append(pairing(edge_b, "row", True))
        accs.append(
            kernel_call(
                block_own_body,
                sds(shape, F32),
                (12 * share * macs, 4 * MIB),
                16,
                vmem=3,
                name="block_own",
            )(attended, activated, block_conv)
        )
    return kernel_call(
        functools.partial(block_edge_body, halves),
        sds(latents.shape, BF),
        (6 * frames_dev * macs, 4 * MIB),
        20,
        vmem=3 * halves + 1,
        name="block_edge",
    )(*accs, *near, *far, block_conv)


def solution(mesh):
    image = P(("group", "frame"), "row", None, None)
    placed = (image, image, P("group"), P("group")) + (P(),) * 9
    return jax.shard_map(shards, mesh=mesh, in_specs=placed, out_specs=image, check_vma=False)
```

time: 60.9 us -> 50.6 us (0.83)
  waiting for transfers between devices: 20.3 us -> 11.4 us
  Pallas kernels: 19.8 us -> 13.2 us
  starting transfers between devices: 14.6 us -> 18.8 us
  local copies, waits for them, and re-layouts: 5.59 us -> 6.39 us
    pallas_call x4 -> x8, Pallas kernels: 19.5 us -> 12.9 us  [the longest x1 5.58 us: shards(): kernel_call(functools.partial(attention_body, n), [sds((share, pix, chann...]
    ppermute x4 -> x6, waiting for transfers between devices: 9.18 us -> 2.92 us  [pairing(): return lax.ppermute(x, axis, pairs)]
    ppermute x9 -> x12, waiting for transfers between devices: 11.1 us -> 8.47 us  [swap(): return lax.ppermute(x, axis, pairs)]
    ppermute x4 -> x6, starting transfers between devices: 8.82 us -> 11.2 us  [pairing(): return lax.ppermute(x, axis, pairs)]
    ppermute x9 -> x12, starting transfers between devices: 5.76 us -> 7.63 us  [swap(): return lax.ppermute(x, axis, pairs)]
    another operation x0 -> x3, local copies, waits for them, and re-layouts: none -> 0.78 us  [the longest x2 0.66 us: shards(): code = positions(frames, channels).reshape(n, frames_dev, channels)]
  transfers between devices with their start and end apart: 13 -> 18, of which waited for: 7 -> 8; matrix products, arithmetic and copies ran while one was open for 0% -> 2% of each run, Pallas kernels for 3% -> 11%
where the time goes in v2:
time: 50.6 us; the launch traced here: 50.2 us
  starting transfers between devices  18.8 us (37%)
  Pallas kernels  13.2 us (26%)
  waiting for transfers between devices  11.4 us (23%)
  local copies, waits for them, and re-layouts  6.39 us (13%)
    ppermute x6, starting transfers between devices, pairing(): return lax.ppermute(x, axis, pairs)  11.2 us
    ppermute x12, waiting for transfers between devices, swap(): return lax.ppermute(x, axis, pairs)  8.47 us
    ppermute x12, starting transfers between devices, swap(): return lax.ppermute(x, axis, pairs)  7.63 us
    unnamed x28, local copies, waits for them, and re-layouts  5.61 us
    pallas_call x1, Pallas kernels, shards(): kernel_call(functools.partial(attention_body, n), [sds((share, pix, chann...  5.58 us
    ppermute x6, waiting for transfers between devices, pairing(): return lax.ppermute(x, axis, pairs)  2.92 us
    pallas_call x1, Pallas kernels, shards(): kernel_call(functools.partial(block_edge_body, halves), sds(latents.shape...  2.02 us
    pallas_call x2, Pallas kernels, shards(): kernel_call(block_own_body, sds(shape, F32), (12 * share * macs, 4 * MIB)...  1.93 us
  transfers between devices with their start and end apart: 18, of which 8 were waited for; matrix products, arithmetic and copies ran while one was open for 2% of the time, Pallas kernels for 11%

profile of v2, /device:TPU:8, one launch (start us, length us, event | category | flops | bytes accessed | tf_op | source)
XLA Modules:
  0.0 50.2 jit_solution(12477942551212175986)
XLA Ops:
  0.0 1.0 %copy-done.2 = bf16[3,2,64,320]{3,2,1,0:T(8,128)(2,1)S(1)} copy-done((bf16[3,2,64,320]{3,2,1,0:T(8,128)(2,1)S(1)}, bf16[3,2,64,320]{3,2,1,0:T(8,128)(2,1)}, u32[]{:S(2)}) %copy-start.2) | copy-done | bytes 245784
  1.0 1.1 %copy-done.4 = bf16[6,2,64,320]{3,2,1,0:T(8,128)(2,1)S(1)} copy-done((bf16[6,2,64,320]{3,2,1,0:T(8,128)(2,1)S(1)}, bf16[6,2,64,320]{3,2,1,0:T(8,128)(2,1)}, u32[]{:S(2)}) %copy-start.4) | copy-done | bytes 491544
  2.4 1.6 %collective-permute-start.1 = (bf16[6,2,16,320]{3,2,1,0:T(8,128)(2,1)S(1)}, bf16[6,2,16,320]{3,2,1,0:T(8,128)(2,1)S(1)}, u32[]{:S(2)}, u32[]{:S(2)}) collective-permute-start(bf16[6,2,16,320]{3,2,1,0:T(8,128)(2,1)S(1)} %get-tuple-element.36), channel_id=1, source_target_pairs={{0,8},{4,12},{8,0},{12,4},{1,9},{5,13},{9,1},{13,5},{2,10},{6,14},... | collective-permute-start | bytes 368648 | tf_op jit(solution)/shard_map/ppermute | solution.py:100
  4.5 4.8 %collective-permute-start.4 = (bf16[3,64,320]{2,1,0:T(8,128)(2,1)S(1)}, bf16[3,64,320]{2,1,0:T(8,128)(2,1)S(1)}, u32[]{:S(2)}, u32[]{:S(2)}) collective-permute-start(bf16[3,64,320]{2,1,0:T(8,128)(2,1)S(1)} %get-tuple-element.40), channel_id=1, source_target_pairs={{1,2},{2,1},{5,6},{6,5},{9,10},{10,9},{13,14},{14,13},{17,18},{18,... | collective-permute-start | bytes 368648 | tf_op jit(solution)/shard_map/ppermute | solution.py:110
  9.4 1.6 %copy-done.1 = bf16[9,320,320]{2,1,0:T(8,128)(2,1)S(1)} copy-done((bf16[9,320,320]{2,1,0:T(8,128)(2,1)S(1)}, bf16[9,320,320]{2,1,0:T(8,128)(2,1)}, u32[]{:S(2)}) %copy-start.1) | copy-done | bytes 1843224
  11.0 1.0 %copy-done.3 = bf16[3,2,64,320]{3,2,1,0:T(8,128)(2,1)S(1)} copy-done((bf16[3,2,64,320]{3,2,1,0:T(8,128)(2,1)S(1)}, bf16[3,2,64,320]{3,2,1,0:T(8,128)(2,1)}, u32[]{:S(2)}) %copy-start.3) | copy-done | bytes 245784
  12.0 0.9 %copy-done.5 = bf16[320,320]{1,0:T(8,128)(2,1)S(1)} copy-done((bf16[320,320]{1,0:T(8,128)(2,1)S(1)}, bf16[320,320]{1,0:T(8,128)(2,1)}, u32[]{:S(2)}) %copy-start.5) | copy-done | bytes 204824
  12.9 1.6 %encoder_own.1 = (f32[2,192,320]{2,1,0:T(8,128)S(1)}, bf16[9,320,320]{2,1,0:T(8,128)(2,1)S(1)}, bf16[320,320]{1,0:T(8,128)(2,1)S(1)}) custom-call(bf16[3,2,64,320]{3,2,1,0:T(8,128)(2,1)S(1)} %copy-done.3, bf16[9,320,320]{2,1,0:T(8,128)(2,1)S(1)} %copy-done.1, bf16[320,320]{1,0:T(8,128)(2,1)S(1)} %copy-done.5), custom_call_target="tpu_custom_call" | custom-call | flops 471859200 | bytes 4194304 | tf_op jit(solution)/shard_map/encoder_own/pallas_call | solution.py:389
  14.7 1.1 %encoder_edge.1 = (bf16[3,2,16,320]{3,2,1,0:T(8,128)(2,1)S(1)}, bf16[3,2,16,320]{3,2,1,0:T(8,128)(2,1)S(1)}, bf16[3,2,16,320]{3,2,1,0:T(8,128)(2,1)S(1)}, bf16[3,2,16,320]{3,2,1,0:T(8,128)(2,1)S(1)}) custom-call(f32[2,192,320]{2,1,0:T(8,128)S(1)} %get-tuple-element.38.acc_ref, bf16[3,64,320]{2,1,0:T(8,128)(2,1)S(1)} %collective-permute-done.3.ha_ref, ...), custom_call_target="tpu_custom_call" | custom-call | flops 314572800 | bytes 4194304 | tf_op jit(solution)/shard_map/encoder_edge/pallas_call | solution.py:402
  15.8 1.6 %collective-permute-start.6 = (bf16[3,2,16,320]{3,2,1,0:T(8,128)(2,1)S(1)}, bf16[3,2,16,320]{3,2,1,0:T(8,128)(2,1)S(1)}, u32[]{:S(2)}, u32[]{:S(2)}) collective-permute-start(bf16[3,2,16,320]{3,2,1,0:T(8,128)(2,1)S(1)} %get-tuple-element.45), channel_id=1, source_target_pairs={{0,8},{4,12},{8,0},{12,4},{1,9},{5,13},{9,1},{13,5},{2,10},{6,14},... | collective-permute-start | bytes 184328 | tf_op jit(solution)/shard_map/ppermute | solution.py:100
  17.8 0.4 reshape_reshape.3
  18.2 0.3 copy.16.refs_8_
  18.5 2.1 %collective-permute-done.6 = bf16[3,2,16,320]{3,2,1,0:T(8,128)(2,1)S(1)} collective-permute-done((bf16[3,2,16,320]{3,2,1,0:T(8,128)(2,1)S(1)}, bf16[3,2,16,320]{3,2,1,0:T(8,128)(2,1)S(1)}, u32[]{:S(2)}, u32[]{:S(2)}) %collective-permute-start.6) | collective-permute-done | bytes 61472 | tf_op jit(solution)/shard_map/ppermute | solution.py:100
  20.6 1.3 %collective-permute-done.7 = bf16[3,2,16,320]{3,2,1,0:T(8,128)(2,1)S(1)} collective-permute-done((bf16[3,2,16,320]{3,2,1,0:T(8,128)(2,1)S(1)}, bf16[3,2,16,320]{3,2,1,0:T(8,128)(2,1)S(1)}, u32[]{:S(2)}, u32[]{:S(2)}) %collective-permute-start.7) | collective-permute-done | bytes 61472 | tf_op jit(solution)/shard_map/ppermute | solution.py:100
  21.9 5.6 %attention.1 = (bf16[3,32,320]{2,1,0:T(8,128)(2,1)S(1)}, bf16[3,32,320]{2,1,0:T(8,128)(2,1)S(1)}, bf16[3,32,320]{2,1,0:T(8,128)(2,1)S(1)}, bf16[3,32,320]{2,1,0:...) custom-call(s32[12]{0:T(128)S(1)} %copy-done.12, ...), custom_call_target="tpu_custom_call" | custom-call | flops 1258291200 | bytes 4194304 | tf_op jit(solution)/shard_map/attention/pallas_call | solution.py:420
  27.7 1.5 %collective-permute-start.9 = (bf16[3,2,16,320]{3,2,1,0:T(8,128)(2,1)S(1)}, bf16[3,2,16,320]{3,2,1,0:T(8,128)(2,1)S(1)}, u32[]{:S(2)}, u32[]{:S(2)}) collective-permute-start(bf16[3,2,16,320]{3,2,1,0:T(8,128)(2,1)S(1)} %bitcast.32), channel_id=1, source_target_pairs={{0,8},{4,12},{8,0},{12,4},{1,9},{5,13},{9,1},{13,5},{2,10},{6,14},... | collective-permute-start | bytes 184328 | tf_op jit(solution)/shard_map/ppermute | solution.py:100
  29.1 0.3 collective-permute-start.10
  29.4 0.4 collective-permute-start.11
  29.8 1.5 %collective-permute-start.12 = (bf16[3,2,16,320]{3,2,1,0:T(8,128)(2,1)S(1)}, bf16[3,2,16,320]{3,2,1,0:T(8,128)(2,1)S(1)}, u32[]{:S(2)}, u32[]{:S(2)}) collective-permute-start(bf16[3,2,16,320]{3,2,1,0:T(8,128)(2,1)S(1)} %bitcast.26), channel_id=1, source_target_pairs={{0,8},{4,12},{8,0},{12,4},{1,9},{5,13},{9,1},{13,5},{2,10},{6,14},... | collective-permute-start | bytes 184328 | tf_op jit(solution)/shard_map/ppermute | solution.py:100
  31.3 1.1 %collective-permute-done.9.refs_2_ = bf16[3,2,16,320]{3,2,1,0:T(8,128)(2,1)S(1)} collective-permute-done((bf16[3,2,16,320]{3,2,1,0:T(8,128)(2,1)S(1)}, bf16[3,2,16,320]{3,2,1,0:T(8,128)(2,1)S(1)}, u32[]{:S(2)}, u32[]{:S(2)}) %collective-permute-start.9) | collective-permute-done | bytes 61472 | tf_op jit(solution)/shard_map/ppermute | solution.py:100
  32.4 1.4 %collective-permute-done.10.refs_3_ = bf16[3,2,16,320]{3,2,1,0:T(8,128)(2,1)S(1)} collective-permute-done((bf16[3,2,16,320]{3,2,1,0:T(8,128)(2,1)S(1)}, bf16[3,2,16,320]{3,2,1,0:T(8,128)(2,1)S(1)}, u32[]{:S(2)}, u32[]{:S(2)}) %collective-permute-start.10) | collective-permute-done | bytes 61472 | tf_op jit(solution)/shard_map/ppermute | solution.py:100
  33.7 0.3 activation.2
  34.2 1.4 %collective-permute-done.12.refs_2_ = bf16[3,2,16,320]{3,2,1,0:T(8,128)(2,1)S(1)} collective-permute-done((bf16[3,2,16,320]{3,2,1,0:T(8,128)(2,1)S(1)}, bf16[3,2,16,320]{3,2,1,0:T(8,128)(2,1)S(1)}, u32[]{:S(2)}, u32[]{:S(2)}) %collective-permute-start.12) | collective-permute-done | bytes 61472 | tf_op jit(solution)/shard_map/ppermute | solution.py:100
  35.5 1.4 %collective-permute-done.13.refs_3_ = bf16[3,2,16,320]{3,2,1,0:T(8,128)(2,1)S(1)} collective-permute-done((bf16[3,2,16,320]{3,2,1,0:T(8,128)(2,1)S(1)}, bf16[3,2,16,320]{3,2,1,0:T(8,128)(2,1)S(1)}, u32[]{:S(2)}, u32[]{:S(2)}) %collective-permute-start.13) | collective-permute-done | bytes 61472 | tf_op jit(solution)/shard_map/ppermute | solution.py:100
  36.9 0.3 activation.3
  37.3 2.4 %collective-permute-start.16 = (bf16[3,64,320]{2,1,0:T(8,128)(2,1)S(1)}, bf16[3,64,320]{2,1,0:T(8,128)(2,1)S(1)}, u32[]{:S(2)}, u32[]{:S(2)}) collective-permute-start(bf16[3,64,320]{2,1,0:T(8,128)(2,1)S(1)} %get-tuple-element.61), channel_id=1, source_target_pairs={{1,2},{2,1},{5,6},{6,5},{9,10},{10,9},{13,14},{14,13},{17,18},{18,... | collective-permute-start | bytes 368648 | tf_op jit(solution)/shard_map/ppermute | solution.py:110
  39.7 3.7 %collective-permute-start.17 = (bf16[3,64,320]{2,1,0:T(8,128)(2,1)S(1)}, bf16[3,64,320]{2,1,0:T(8,128)(2,1)S(1)}, u32[]{:S(2)}, u32[]{:S(2)}) collective-permute-start(bf16[3,64,320]{2,1,0:T(8,128)(2,1)S(1)} %get-tuple-element.62), channel_id=1, source_target_pairs={{1,2},{2,1},{5,6},{6,5},{9,10},{10,9},{13,14},{14,13},{17,18},{18,... | collective-permute-start | bytes 368648 | tf_op jit(solution)/shard_map/ppermute | solution.py:110
  43.4 1.0 %block_own.2.refs_0_ = f32[3,2,64,320]{3,2,1,0:T(8,128)S(1)} custom-call(bf16[3,2,64,320]{3,2,1,0:T(8,128)(2,1)S(1)} %get-tuple-element.51.att_ref, bf16[3,2,64,320]{3,2,1,0:T(8,128)(2,1)S(1)} %get-tuple-element.52.act_ref, bf16[9,320,320]{2,1,0:T(8,128)(2,1)S(1)} %copy-done), custom_call_target="tpu_custom_call" | custom-call | flops 471859200 | bytes 4194304 | tf_op jit(solution)/shard_map/block_own/pallas_call | solution.py:471
  44.3 1.0 %block_own.3.refs_1_ = f32[3,2,64,320]{3,2,1,0:T(8,128)S(1)} custom-call(bf16[3,2,64,320]{3,2,1,0:T(8,128)(2,1)S(1)} %get-tuple-element.57.att_ref, bf16[3,2,64,320]{3,2,1,0:T(8,128)(2,1)S(1)} %get-tuple-element.58.act_ref, bf16[9,320,320]{2,1,0:T(8,128)(2,1)S(1)} %copy-done), custom_call_target="tpu_custom_call" | custom-call | flops 471859200 | bytes 4194304 | tf_op jit(solution)/shard_map/block_own/pallas_call | solution.py:471
  45.3 0.6 %collective-permute-done.16.refs_4_ = bf16[3,64,320]{2,1,0:T(8,128)(2,1)S(1)} collective-permute-done((bf16[3,64,320]{2,1,0:T(8,128)(2,1)S(1)}, bf16[3,64,320]{2,1,0:T(8,128)(2,1)S(1)}, u32[]{:S(2)}, u32[]{:S(2)}) %collective-permute-start.16) | collective-permute-done | bytes 122912 | tf_op jit(solution)/shard_map/ppermute | solution.py:110
  45.9 2.3 %collective-permute-done.17.refs_5_ = bf16[3,64,320]{2,1,0:T(8,128)(2,1)S(1)} collective-permute-done((bf16[3,64,320]{2,1,0:T(8,128)(2,1)S(1)}, bf16[3,64,320]{2,1,0:T(8,128)(2,1)S(1)}, u32[]{:S(2)}, u32[]{:S(2)}) %collective-permute-start.17) | collective-permute-done | bytes 122912 | tf_op jit(solution)/shard_map/ppermute | solution.py:110
  48.2 2.0 %block_edge.1 = bf16[6,2,64,320]{3,2,1,0:T(8,128)(2,1)} custom-call(f32[3,2,64,320]{3,2,1,0:T(8,128)S(1)} %block_own.2.refs_0_, f32[3,2,64,320]{3,2,1,0:T(8,128)S(1)} %block_own.3.refs_1_, bf16[3,64,320]{2,1,0:T(8,128)(2,1)S(1)} %collective-permute-done.14.refs_2_, bf16[3,64,320]{2,1,0:T(8,128)(2,1)S(1)} %collective-permute-done.15.refs_3_, ...), custom_call_target="tpu_custom_call" | custom-call | flops 471859200 | bytes 4194304 | tf_op jit(solution)/shard_map/block_edge/pallas_call | solution.py:480
  (47 shorter events, 1.8 us)
Async XLA Ops:
  0.0 1.0 %copy-start.2 = (bf16[3,2,64,320]{3,2,1,0:T(8,128)(2,1)S(1)}, bf16[3,2,64,320]{3,2,1,0:T(8,128)(2,1)}, u32[]{:S(2)}) copy-start(bf16[3,2,64,320]{3,2,1,0:T(8,128)(2,1)} %cond_hbm.1) | copy-start | bytes 737284
  1.0 1.1 %copy-start.4 = (bf16[6,2,64,320]{3,2,1,0:T(8,128)(2,1)S(1)}, bf16[6,2,64,320]{3,2,1,0:T(8,128)(2,1)}, u32[]{:S(2)}) copy-start(bf16[6,2,64,320]{3,2,1,0:T(8,128)(2,1)} %lat_ref.1) | copy-start | bytes 1474564
  2.3 15.1 %collective-permute-start = (bf16[6,2,16,320]{3,2,1,0:T(8,128)(2,1)S(1)}, bf16[6,2,16,320]{3,2,1,0:T(8,128)(2,1)S(1)}, u32[]{:S(2)}, u32[]{:S(2)}) collective-permute-start(bf16[6,2,16,320]{3,2,1,0:T(8,128)(2,1)S(1)} %get-tuple-element.35), channel_id=1, source_target_pairs={{0,4},{4,0},{8,12},{12,8},{1,5},{5,1},{9,13},{13,9},{2,6},{6,2},{1... | collective-permute-start | bytes 368648 | tf_op jit(solution)/shard_map/ppermute | solution.py:100
  2.4 16.1 %collective-permute-start.1 = (bf16[6,2,16,320]{3,2,1,0:T(8,128)(2,1)S(1)}, bf16[6,2,16,320]{3,2,1,0:T(8,128)(2,1)S(1)}, u32[]{:S(2)}, u32[]{:S(2)}) collective-permute-start(bf16[6,2,16,320]{3,2,1,0:T(8,128)(2,1)S(1)} %get-tuple-element.36), channel_id=1, source_target_pairs={{0,8},{4,12},{8,0},{12,4},{1,9},{5,13},{9,1},{13,5},{2,10},{6,14},... | collective-permute-start | bytes 368648 | tf_op jit(solution)/shard_map/ppermute | solution.py:100
  4.0 14.5 %collective-permute-start.2 = (bf16[6,2,16,320]{3,2,1,0:T(8,128)(2,1)S(1)}, bf16[6,2,16,320]{3,2,1,0:T(8,128)(2,1)S(1)}, u32[]{:S(2)}, u32[]{:S(2)}) collective-permute-start(bf16[6,2,16,320]{3,2,1,0:T(8,128)(2,1)S(1)} %get-tuple-element.37), channel_id=1, source_target_pairs={{0,12},{4,8},{8,4},{12,0},{1,13},{5,9},{9,5},{13,1},{2,14},{6,10},... | collective-permute-start | bytes 368648 | tf_op jit(solution)/shard_map/ppermute | solution.py:100
  4.2 10.3 %collective-permute-start.3 = (bf16[3,64,320]{2,1,0:T(8,128)(2,1)S(1)}, bf16[3,64,320]{2,1,0:T(8,128)(2,1)S(1)}, u32[]{:S(2)}, u32[]{:S(2)}) collective-permute-start(bf16[3,64,320]{2,1,0:T(8,128)(2,1)S(1)} %get-tuple-element.39), channel_id=1, source_target_pairs={{0,1},{1,0},{2,3},{3,2},{4,5},{5,4},{6,7},{7,6},{8,9},{9,8},{10,11... | collective-permute-start | bytes 368648 | tf_op jit(solution)/shard_map/ppermute | solution.py:110
  4.5 10.1 %collective-permute-start.4 = (bf16[3,64,320]{2,1,0:T(8,128)(2,1)S(1)}, bf16[3,64,320]{2,1,0:T(8,128)(2,1)S(1)}, u32[]{:S(2)}, u32[]{:S(2)}) collective-permute-start(bf16[3,64,320]{2,1,0:T(8,128)(2,1)S(1)} %get-tuple-element.40), channel_id=1, source_target_pairs={{1,2},{2,1},{5,6},{6,5},{9,10},{10,9},{13,14},{14,13},{17,18},{18,... | collective-permute-start | bytes 368648 | tf_op jit(solution)/shard_map/ppermute | solution.py:110
  9.4 1.6 %copy-start.1 = (bf16[9,320,320]{2,1,0:T(8,128)(2,1)S(1)}, bf16[9,320,320]{2,1,0:T(8,128)(2,1)}, u32[]{:S(2)}) copy-start(bf16[9,320,320]{2,1,0:T(8,128)(2,1)} %w_hbm.1) | copy-start | bytes 5529604
  11.0 1.0 %copy-start.3 = (bf16[3,2,64,320]{3,2,1,0:T(8,128)(2,1)S(1)}, bf16[3,2,64,320]{3,2,1,0:T(8,128)(2,1)}, u32[]{:S(2)}) copy-start(bf16[3,2,64,320]{3,2,1,0:T(8,128)(2,1)} %cond_hbm.1) | copy-start | bytes 737284
  12.0 0.9 %copy-start.5 = (bf16[320,320]{1,0:T(8,128)(2,1)S(1)}, bf16[320,320]{1,0:T(8,128)(2,1)}, u32[]{:S(2)}) copy-start(bf16[320,320]{1,0:T(8,128)(2,1)} %zero_hbm.1) | copy-start | bytes 614404
  14.6 7.2 %copy-start.7 = (bf16[320,320]{1,0:T(8,128)(2,1)S(1)}, bf16[320,320]{1,0:T(8,128)(2,1)}, u32[]{:S(2)}) copy-start(bf16[320,320]{1,0:T(8,128)(2,1)} %refs_10_.1) | copy-start | bytes 614404
  14.6 7.2 %copy-start.8 = (bf16[320,320]{1,0:T(8,128)(2,1)S(1)}, bf16[320,320]{1,0:T(8,128)(2,1)}, u32[]{:S(2)}) copy-start(bf16[320,320]{1,0:T(8,128)(2,1)} %refs_11_.1) | copy-start | bytes 614404
  14.6 7.2 %copy-start.9 = (bf16[320,320]{1,0:T(8,128)(2,1)S(1)}, bf16[320,320]{1,0:T(8,128)(2,1)}, u32[]{:S(2)}) copy-start(bf16[320,320]{1,0:T(8,128)(2,1)} %refs_12_.1) | copy-start | bytes 614404
  14.6 7.2 %copy-start.10 = (bf16[320,320]{1,0:T(8,128)(2,1)S(1)}, bf16[320,320]{1,0:T(8,128)(2,1)}, u32[]{:S(2)}) copy-start(bf16[320,320]{1,0:T(8,128)(2,1)} %refs_13_.1) | copy-start | bytes 614404
  14.6 7.2 %copy-start.11 = (f32[320]{0:T(512)S(1)}, f32[320]{0:T(512)}, u32[]{:S(2)}) copy-start(f32[320]{0:T(512)} %refs_9_.1) | copy-start | bytes 3844
  14.7 7.2 %copy-start.12 = (s32[12]{0:T(128)S(1)}, s32[12]{0:T(128)}, u32[]{:S(2)}) copy-start(s32[12]{0:T(128)} %kf_ref.1) | copy-start | bytes 148
  14.7 7.2 %copy-start.13 = (s32[24]{0:T(128)S(1)}, s32[24]{0:T(128)}, u32[]{:S(2)}) copy-start(s32[24]{0:T(128)} %prop_ref.1) | copy-start | bytes 292
  15.7 2.8 %collective-permute-start.5 = (bf16[3,2,16,320]{3,2,1,0:T(8,128)(2,1)S(1)}, bf16[3,2,16,320]{3,2,1,0:T(8,128)(2,1)S(1)}, u32[]{:S(2)}, u32[]{:S(2)}) collective-permute-start(bf16[3,2,16,320]{3,2,1,0:T(8,128)(2,1)S(1)} %get-tuple-element.44), channel_id=1, source_target_pairs={{0,4},{4,0},{8,12},{12,8},{1,5},{5,1},{9,13},{13,9},{2,6},{6,2},{1... | collective-permute-start | bytes 184328 | tf_op jit(solution)/shard_map/ppermute | solution.py:100
  15.8 4.8 %collective-permute-start.6 = (bf16[3,2,16,320]{3,2,1,0:T(8,128)(2,1)S(1)}, bf16[3,2,16,320]{3,2,1,0:T(8,128)(2,1)S(1)}, u32[]{:S(2)}, u32[]{:S(2)}) collective-permute-start(bf16[3,2,16,320]{3,2,1,0:T(8,128)(2,1)S(1)} %get-tuple-element.45), channel_id=1, source_target_pairs={{0,8},{4,12},{8,0},{12,4},{1,9},{5,13},{9,1},{13,5},{2,10},{6,14},... | collective-permute-start | bytes 184328 | tf_op jit(solution)/shard_map/ppermute | solution.py:100
  17.4 4.4 %collective-permute-start.7 = (bf16[3,2,16,320]{3,2,1,0:T(8,128)(2,1)S(1)}, bf16[3,2,16,320]{3,2,1,0:T(8,128)(2,1)S(1)}, u32[]{:S(2)}, u32[]{:S(2)}) collective-permute-start(bf16[3,2,16,320]{3,2,1,0:T(8,128)(2,1)S(1)} %get-tuple-element.46), channel_id=1, source_target_pairs={{0,12},{4,8},{8,4},{12,0},{1,13},{5,9},{9,5},{13,1},{2,14},{6,10},... | collective-permute-start | bytes 184328 | tf_op jit(solution)/shard_map/ppermute | solution.py:100
  21.9 11.8 %copy-start.6 = (f32[320]{0:T(512)S(1)}, f32[320]{0:T(512)}, u32[]{:S(2)}) copy-start(f32[320]{0:T(512)} %refs_4_.3) | copy-start | bytes 3844
  21.9 21.4 %copy-start = (bf16[9,320,320]{2,1,0:T(8,128)(2,1)S(1)}, bf16[9,320,320]{2,1,0:T(8,128)(2,1)}, u32[]{:S(2)}) copy-start(bf16[9,320,320]{2,1,0:T(8,128)(2,1)} %refs_6_.1) | copy-start | bytes 5529604
  27.5 3.8 %collective-permute-start.8 = (bf16[3,2,16,320]{3,2,1,0:T(8,128)(2,1)S(1)}, bf16[3,2,16,320]{3,2,1,0:T(8,128)(2,1)S(1)}, u32[]{:S(2)}, u32[]{:S(2)}) collective-permute-start(bf16[3,2,16,320]{3,2,1,0:T(8,128)(2,1)S(1)} %bitcast.33), channel_id=1, source_target_pairs={{0,4},{4,0},{8,12},{12,8},{1,5},{5,1},{9,13},{13,9},{2,6},{6,2},{1... | collective-permute-start | bytes 184328 | tf_op jit(solution)/shard_map/ppermute | solution.py:100
  27.7 4.7 %collective-permute-start.9 = (bf16[3,2,16,320]{3,2,1,0:T(8,128)(2,1)S(1)}, bf16[3,2,16,320]{3,2,1,0:T(8,128)(2,1)S(1)}, u32[]{:S(2)}, u32[]{:S(2)}) collective-permute-start(bf16[3,2,16,320]{3,2,1,0:T(8,128)(2,1)S(1)} %bitcast.32), channel_id=1, source_target_pairs={{0,8},{4,12},{8,0},{12,4},{1,9},{5,13},{9,1},{13,5},{2,10},{6,14},... | collective-permute-start | bytes 184328 | tf_op jit(solution)/shard_map/ppermute | solution.py:100
  29.1 4.6 %collective-permute-start.10 = (bf16[3,2,16,320]{3,2,1,0:T(8,128)(2,1)S(1)}, bf16[3,2,16,320]{3,2,1,0:T(8,128)(2,1)S(1)}, u32[]{:S(2)}, u32[]{:S(2)}) collective-permute-start(bf16[3,2,16,320]{3,2,1,0:T(8,128)(2,1)S(1)} %bitcast.31), channel_id=1, source_target_pairs={{0,12},{4,8},{8,4},{12,0},{1,13},{5,9},{9,5},{13,1},{2,14},{6,10},... | collective-permute-start | bytes 184328 | tf_op jit(solution)/shard_map/ppermute | solution.py:100
  29.4 4.7 %collective-permute-start.11 = (bf16[3,2,16,320]{3,2,1,0:T(8,128)(2,1)S(1)}, bf16[3,2,16,320]{3,2,1,0:T(8,128)(2,1)S(1)}, u32[]{:S(2)}, u32[]{:S(2)}) collective-permute-start(bf16[3,2,16,320]{3,2,1,0:T(8,128)(2,1)S(1)} %bitcast.27), channel_id=1, source_target_pairs={{0,4},{4,0},{8,12},{12,8},{1,5},{5,1},{9,13},{13,9},{2,6},{6,2},{1... | collective-permute-start | bytes 184328 | tf_op jit(solution)/shard_map/ppermute | solution.py:100
  29.8 5.7 %collective-permute-start.12 = (bf16[3,2,16,320]{3,2,1,0:T(8,128)(2,1)S(1)}, bf16[3,2,16,320]{3,2,1,0:T(8,128)(2,1)S(1)}, u32[]{:S(2)}, u32[]{:S(2)}) collective-permute-start(bf16[3,2,16,320]{3,2,1,0:T(8,128)(2,1)S(1)} %bitcast.26), channel_id=1, source_target_pairs={{0,8},{4,12},{8,0},{12,4},{1,9},{5,13},{9,1},{13,5},{2,10},{6,14},... | collective-permute-start | bytes 184328 | tf_op jit(solution)/shard_map/ppermute | solution.py:100
  31.3 5.6 %collective-permute-start.13 = (bf16[3,2,16,320]{3,2,1,0:T(8,128)(2,1)S(1)}, bf16[3,2,16,320]{3,2,1,0:T(8,128)(2,1)S(1)}, u32[]{:S(2)}, u32[]{:S(2)}) collective-permute-start(bf16[3,2,16,320]{3,2,1,0:T(8,128)(2,1)S(1)} %bitcast.24), channel_id=1, source_target_pairs={{0,12},{4,8},{8,4},{12,0},{1,13},{5,9},{9,5},{13,1},{2,14},{6,10},... | collective-permute-start | bytes 184328 | tf_op jit(solution)/shard_map/ppermute | solution.py:100
  34.1 11.2 %collective-permute-start.14 = (bf16[3,64,320]{2,1,0:T(8,128)(2,1)S(1)}, bf16[3,64,320]{2,1,0:T(8,128)(2,1)S(1)}, u32[]{:S(2)}, u32[]{:S(2)}) collective-permute-start(bf16[3,64,320]{2,1,0:T(8,128)(2,1)S(1)} %get-tuple-element.59), channel_id=1, source_target_pairs={{0,1},{1,0},{2,3},{3,2},{4,5},{5,4},{6,7},{7,6},{8,9},{9,8},{10,11... | collective-permute-start | bytes 368648 | tf_op jit(solution)/shard_map/ppermute | solution.py:110
  37.2 8.1 %collective-permute-start.15 = (bf16[3,64,320]{2,1,0:T(8,128)(2,1)S(1)}, bf16[3,64,320]{2,1,0:T(8,128)(2,1)S(1)}, u32[]{:S(2)}, u32[]{:S(2)}) collective-permute-start(bf16[3,64,320]{2,1,0:T(8,128)(2,1)S(1)} %get-tuple-element.60), channel_id=1, source_target_pairs={{0,1},{1,0},{2,3},{3,2},{4,5},{5,4},{6,7},{7,6},{8,9},{9,8},{10,11... | collective-permute-start | bytes 368648 | tf_op jit(solution)/shard_map/ppermute | solution.py:110
  37.3 8.6 %collective-permute-start.16 = (bf16[3,64,320]{2,1,0:T(8,128)(2,1)S(1)}, bf16[3,64,320]{2,1,0:T(8,128)(2,1)S(1)}, u32[]{:S(2)}, u32[]{:S(2)}) collective-permute-start(bf16[3,64,320]{2,1,0:T(8,128)(2,1)S(1)} %get-tuple-element.61), channel_id=1, source_target_pairs={{1,2},{2,1},{5,6},{6,5},{9,10},{10,9},{13,14},{14,13},{17,18},{18,... | collective-permute-start | bytes 368648 | tf_op jit(solution)/shard_map/ppermute | solution.py:110
  39.7 8.5 %collective-permute-start.17 = (bf16[3,64,320]{2,1,0:T(8,128)(2,1)S(1)}, bf16[3,64,320]{2,1,0:T(8,128)(2,1)S(1)}, u32[]{:S(2)}, u32[]{:S(2)}) collective-permute-start(bf16[3,64,320]{2,1,0:T(8,128)(2,1)S(1)} %get-tuple-element.62), channel_id=1, source_target_pairs={{1,2},{2,1},{5,6},{6,5},{9,10},{10,9},{13,14},{14,13},{17,18},{18,... | collective-permute-start | bytes 368648 | tf_op jit(solution)/shard_map/ppermute | solution.py:110
